TPU v7x, 32 devices: a whole 2x2x4 slice. The times are simulated.
32 devices in a mesh: rows: 4 (over y, core), cols: 8 (over z, x).
Axes of the slice: x: 2, y: 2, z: 4, core: 2. Of those that a mesh axis runs over, the one named last changes fastest.
Arguments:
- prior: float32 [64, 512, 512], P('rows', 'cols'), may hold values from -6 to 6
- obs_cell: int32 [8, 128], replicated, may hold values from 0 to 32767, as said below
- obs_weight: float32 [8, 128, 8], replicated, may hold values from 0.1 to 1
- obs_value: float32 [8, 128], replicated, may hold values from -8 to 8
- obs_var: float32 [8, 128], replicated, may hold values from 0.25 to 4
- loc_mask: int32 [8, 32], replicated, may hold values from 0 to 1, as said below
- batch_order: int32 [8], replicated, may hold values from 0 to 7, each once
- kernel: float32 [8, 7, 7], replicated, may hold values from 0.005 to 0.04
- mixing: float32 [8, 8], replicated, may hold values from -2 to 2
Outputs:
- forecast: float32 [64, 512, 512], P('rows', 'cols')
Inputs may be any that keep to these rules, and one draw needn't show every extreme that they name: `obs_cell`: all 128 cells of one batch lie in one tile, rows r * 16 to (r + 1) * 16 - 1 and columns c * 64 to (c + 1) * 64 - 1, whose index is r * 8 + c. `loc_mask`: for each batch the tiles marked 1 form a rectangle of tiles that contains the tile of that batch's cells. `batch_order`: each batch appears once.
All inputs are finite; a program needn't handle non-finite values.
Results may differ from a plain program's by a relative error of at most 0.0003.
Values sent between devices are 32-bit elements; how exact they have to be, the bound alone decides.
No kernel may reach another device: no remote copies, remote signals or barrier semaphores. Data moves between devices by JAX's collectives and lax.ppermute only.
A program may use at most 128 MiB of HBM per device.

v0:
```python
import jax
import jax.numpy as jnp
from jax import lax
from jax.sharding import PartitionSpec as P

BATCHES = 8
KW = 7
HALFW = 48


def with_halo(shard, sides, width):
    for axis, dim in sides:
        size, length = (lax.axis_size(axis), shard.shape[dim])
        up = [(i, (i + 1) % size) for i in range(size - 1)]
        down = [(j, i) for i, j in up]
        last = lax.slice_in_dim(shard, length - width, length, axis=dim)
        initial = lax.slice_in_dim(shard, 0, width, axis=dim)
        before = lax.ppermute(last, axis, up)
        after = lax.ppermute(initial, axis, down)
        shard = jnp.concatenate([before, shard, after], axis=dim)
    return shard


def taper_weights(ratio):
    clamped = jnp.maximum(ratio, 1.0)
    inner_part = (((-0.25 * ratio + 0.5) * ratio + 0.625) * ratio - 5.0 / 3.0) * ratio * ratio + 1.0
    outer_part = (
        ((((ratio / 12.0 - 0.5) * ratio + 0.625) * ratio + 5.0 / 3.0) * ratio - 5.0) * ratio
        + 4.0
        - 2.0 / (3.0 * clamped)
    )
    return jnp.where(ratio <= 1.0, inner_part, jnp.where(ratio < 2.0, outer_part, 0.0))


def batch_gain(predicted, value_row, var_row):
    mean_pred = jnp.mean(predicted, axis=1)
    spread = predicted - mean_pred[:, None]
    variance = jnp.sum(spread * spread, axis=1) / (predicted.shape[1] - 1)
    denominator = variance + var_row
    shrink = 1.0 / (1.0 + jnp.sqrt(var_row / denominator))
    kalman_gain = ((value_row - mean_pred)[:, None] - shrink[:, None] * spread) / denominator[
        :, None
    ]
    return (spread, kalman_gain)


def refresh_block(block, first_row, first_col, cell_row, cell_col, spread, kalman_gain, active):
    rows_count, cols_count, channels = block.shape
    members = spread.shape[1]
    species = channels // members
    row_pos = (first_row + jnp.arange(rows_count, dtype=jnp.int32)).astype(jnp.float32)
    col_pos = (first_col + jnp.arange(cols_count, dtype=jnp.int32)).astype(jnp.float32)
    row_gap = row_pos[:, None, None] - cell_row.astype(jnp.float32)[None, None, :]
    col_gap = col_pos[None, :, None] - cell_col.astype(jnp.float32)[None, None, :]
    squared = row_gap * row_gap + col_gap * col_gap
    taper = taper_weights(jnp.sqrt(squared) / HALFW) * active
    taper = taper.reshape(rows_count * cols_count, cell_row.shape[0])
    members_view = block.reshape(rows_count * cols_count, species, members)
    covariance = jnp.einsum(
        "psm,im->psi", members_view, spread, precision=lax.Precision.HIGHEST
    ) / (members - 1)
    increment = jnp.einsum(
        "psi,im->psm", covariance * taper[:, None, :], kalman_gain, precision=lax.Precision.HIGHEST
    )
    return (members_view + increment).reshape(rows_count, cols_count, channels)


def refresh_tile(ensemble, row_start, col_start, cell_row, cell_col, spread, kalman_gain, active):
    pieces = refresh_block(
        ensemble, row_start + 0, col_start, cell_row, cell_col, spread, kalman_gain, active
    )
    return pieces


def local_prediction(ensemble, cell_row, cell_col, weights_rows, row_start, col_start):
    tile_height, tile_width, channels = ensemble.shape
    species = weights_rows.shape[1]
    members = channels // species
    local_row = cell_row - row_start
    local_col = cell_col - col_start
    inside = (
        (local_row >= 0) & (local_row < tile_height) & (local_col >= 0) & (local_col < tile_width)
    )
    flat_index = jnp.clip(local_row, 0, tile_height - 1) * tile_width + jnp.clip(
        local_col, 0, tile_width - 1
    )
    picked = ensemble.reshape(tile_height * tile_width, species, members)[flat_index]
    predicted = jnp.einsum("is,ism->im", weights_rows, picked, precision=lax.Precision.HIGHEST)
    return jnp.where(inside[:, None], predicted, 0.0)


def shards(prior, obs_cell, obs_weight, obs_value, obs_var, loc_mask, batch_order, kernel, mixing):
    tile_height, tile_width, channels = prior.shape
    species = kernel.shape[0]
    members = channels // species
    cols_count = lax.axis_size("cols")
    grid_width = tile_width * cols_count
    row_start = lax.axis_index("rows") * tile_height
    col_start = lax.axis_index("cols") * tile_width
    my_tile = lax.axis_index("rows") * cols_count + lax.axis_index("cols")
    ensemble = prior
    for position in range(BATCHES):
        current = batch_order[position]
        obs_cells = obs_cell[current]
        cell_row = obs_cells // grid_width
        cell_col = obs_cells % grid_width
        partial_value = local_prediction(
            ensemble, cell_row, cell_col, obs_weight[current], row_start, col_start
        )
        predicted = lax.psum(partial_value, ("rows", "cols"))
        spread, kalman_gain = batch_gain(predicted, obs_value[current], obs_var[current])
        active = loc_mask[current, my_tile].astype(jnp.float32)
        ensemble = refresh_tile(
            ensemble, row_start, col_start, cell_row, cell_col, spread, kalman_gain, active
        )
    halo_width = KW // 2
    padded = with_halo(ensemble, (("rows", 0), ("cols", 1)), 3)
    padded_width = tile_width + 2 * halo_width
    offsets = (
        jnp.arange(padded_width, dtype=jnp.int32)[None, :]
        - jnp.arange(tile_width, dtype=jnp.int32)[:, None]
    )
    onehot = (offsets[:, :, None] == jnp.arange(KW, dtype=jnp.int32)[None, None, :]).astype(
        jnp.float32
    )
    band_matrix = jnp.einsum("tak,xik->taxi", kernel, onehot, precision=lax.Precision.HIGHEST)
    padded_grid = padded.reshape(tile_height + 2 * halo_width, padded_width, species, members)
    smoothed = jnp.zeros((tile_height, tile_width, species, members), jnp.float32)
    for vertical in range(KW):
        smoothed = smoothed + jnp.einsum(
            "txi,yitm->yxtm",
            band_matrix[:, vertical],
            padded_grid[vertical : vertical + tile_height],
            precision=lax.Precision.HIGHEST,
        )
    mixed_field = jnp.einsum("st,yxtm->yxsm", mixing, smoothed, precision=lax.Precision.HIGHEST)
    return mixed_field.reshape(tile_height, tile_width, channels)


def solution(mesh):
    return jax.shard_map(
        shards,
        mesh=mesh,
        in_specs=(P("rows", "cols", None), P(), P(), P(), P(), P(), P(), P(), P()),
        out_specs=P("rows", "cols", None),
        check_vma=False,
    )
```

profile of v0, /device:TPU:9, one launch (start us, length us, event | category | flops | bytes accessed | tf_op | source)
XLA Modules:
  0.0 676.0 jit_solution(12245388337613379013)
XLA Ops:
  34.7 39.9 %psum.56 = f32[128,64]{0,1:T(8,128)S(1)} all-reduce(f32[128,64]{0,1:T(8,128)S(1)} %broadcast_select_fusion.7), channel_id=1, replica_groups=mesh['rows'=4,'cols'=8] {'rows','cols'}, use_global_device_ids=true, to_apply=%region_0.1 | all-reduce | flops 8192 | bytes 65536 | tf_op jit(solution)/shard_map/psum | solution.py:110
  90.2 39.7 %psum.57 = f32[128,64]{0,1:T(8,128)S(1)} all-reduce(f32[128,64]{0,1:T(8,128)S(1)} %broadcast_select_fusion.6), channel_id=1, replica_groups=mesh['rows'=4,'cols'=8] {'rows','cols'}, use_global_device_ids=true, to_apply=%region_3.4 | all-reduce | flops 8192 | bytes 65536 | tf_op jit(solution)/shard_map/psum | solution.py:110
  130.0 6.8 %fusion.242 = f32[1024,8,128]{2,0,1:T(8,128)S(1)} fusion(f32[1024,8,64]{0,2,1:T(8,128)S(1)} %fusion.60, f32[128,64]{0,1:T(8,128)S(1)} %psum.57, f32[128]{0:T(128)S(1)} %get-tuple-element.169), kind=kOutput, calls=%fused_computation.329 | convolution fusion | flops 805314560 | bytes 6324736 | tf_op jit(solution)/shard_map/psm,im->psi/dot_general | solution.py:59
  138.1 6.3 fusion.39
  151.9 41.2 %psum.58 = f32[128,64]{0,1:T(8,128)S(1)} all-reduce(f32[128,64]{0,1:T(8,128)S(1)} %broadcast_select_fusion.5), channel_id=1, replica_groups=mesh['rows'=4,'cols'=8] {'rows','cols'}, use_global_device_ids=true, to_apply=%region_6.7 | all-reduce | flops 8192 | bytes 65536 | tf_op jit(solution)/shard_map/psum | solution.py:110
  193.2 6.8 %fusion.239 = f32[1024,8,128]{2,0,1:T(8,128)S(1)} fusion(f32[1024,8,64]{0,2,1:T(8,128)S(1)} %copy-done.2, f32[128,64]{0,1:T(8,128)S(1)} %psum.58, f32[128]{0:T(128)S(1)} %get-tuple-element.167), kind=kOutput, calls=%fused_computation.326 | convolution fusion | flops 805314560 | bytes 6324736 | tf_op jit(solution)/shard_map/psm,im->psi/dot_general | solution.py:59
  201.4 6.3 fusion.42
  215.4 39.3 %psum.59 = f32[128,64]{0,1:T(8,128)S(1)} all-reduce(f32[128,64]{0,1:T(8,128)S(1)} %broadcast_select_fusion.4), channel_id=1, replica_groups=mesh['rows'=4,'cols'=8] {'rows','cols'}, use_global_device_ids=true, to_apply=%region_9.10 | all-reduce | flops 8192 | bytes 65536 | tf_op jit(solution)/shard_map/psum | solution.py:110
  254.8 6.8 %fusion.236 = f32[1024,8,128]{2,0,1:T(8,128)S(1)} fusion(f32[1024,8,64]{0,2,1:T(8,128)S(1)} %copy-done.3, f32[128,64]{0,1:T(8,128)S(1)} %psum.59, f32[128]{0:T(128)S(1)} %get-tuple-element.165), kind=kOutput, calls=%fused_computation.323 | convolution fusion | flops 805314560 | bytes 6324736 | tf_op jit(solution)/shard_map/psm,im->psi/dot_general | solution.py:59
  263.0 6.3 fusion.45
  276.8 41.1 %psum.60 = f32[128,64]{0,1:T(8,128)S(1)} all-reduce(f32[128,64]{0,1:T(8,128)S(1)} %broadcast_select_fusion.3), channel_id=1, replica_groups=mesh['rows'=4,'cols'=8] {'rows','cols'}, use_global_device_ids=true, to_apply=%region_12.13 | all-reduce | flops 8192 | bytes 65536 | tf_op jit(solution)/shard_map/psum | solution.py:110
  318.0 6.8 %fusion.233 = f32[1024,8,128]{2,0,1:T(8,128)S(1)} fusion(f32[1024,8,64]{0,2,1:T(8,128)S(1)} %copy-done.4, f32[128,64]{0,1:T(8,128)S(1)} %psum.60, f32[128]{0:T(128)S(1)} %get-tuple-element.163), kind=kOutput, calls=%fused_computation.320 | convolution fusion | flops 805314560 | bytes 6324736 | tf_op jit(solution)/shard_map/psm,im->psi/dot_general | solution.py:59
  326.2 6.3 fusion.48
  340.2 39.3 %psum.61 = f32[128,64]{0,1:T(8,128)S(1)} all-reduce(f32[128,64]{0,1:T(8,128)S(1)} %broadcast_select_fusion.2), channel_id=1, replica_groups=mesh['rows'=4,'cols'=8] {'rows','cols'}, use_global_device_ids=true, to_apply=%region_15.16 | all-reduce | flops 8192 | bytes 65536 | tf_op jit(solution)/shard_map/psum | solution.py:110
  379.6 6.8 %fusion.230 = f32[1024,8,128]{2,0,1:T(8,128)S(1)} fusion(f32[1024,8,64]{0,2,1:T(8,128)S(1)} %copy-done.5, f32[128,64]{0,1:T(8,128)S(1)} %psum.61, f32[128]{0:T(128)S(1)} %get-tuple-element.161), kind=kOutput, calls=%fused_computation.317 | convolution fusion | flops 805314560 | bytes 6324736 | tf_op jit(solution)/shard_map/psm,im->psi/dot_general | solution.py:59
  387.8 6.3 fusion.51
  401.4 41.3 %psum.62 = f32[128,64]{0,1:T(8,128)S(1)} all-reduce(f32[128,64]{0,1:T(8,128)S(1)} %broadcast_select_fusion.1), channel_id=1, replica_groups=mesh['rows'=4,'cols'=8] {'rows','cols'}, use_global_device_ids=true, to_apply=%region_18.19 | all-reduce | flops 8192 | bytes 65536 | tf_op jit(solution)/shard_map/psum | solution.py:110
  442.8 6.8 %fusion.227 = f32[1024,8,128]{2,0,1:T(8,128)S(1)} fusion(f32[1024,8,64]{0,2,1:T(8,128)S(1)} %copy-done.6, f32[128,64]{0,1:T(8,128)S(1)} %psum.62, f32[128]{0:T(128)S(1)} %get-tuple-element.159), kind=kOutput, calls=%fused_computation.314 | convolution fusion | flops 805314560 | bytes 6324736 | tf_op jit(solution)/shard_map/psm,im->psi/dot_general | solution.py:59
  461.9 39.7 %psum.63 = f32[128,64]{0,1:T(8,128)S(1)} all-reduce(f32[128,64]{0,1:T(8,128)S(1)} %broadcast_select_fusion), channel_id=1, replica_groups=mesh['rows'=4,'cols'=8] {'rows','cols'}, use_global_device_ids=true, to_apply=%region_21.22 | all-reduce | flops 8192 | bytes 65536 | tf_op jit(solution)/shard_map/psum | solution.py:110
  501.7 6.8 %fusion.224 = f32[1024,8,128]{2,0,1:T(8,128)S(1)} fusion(f32[1024,8,64]{0,2,1:T(8,128)S(1)} %fusion.54, f32[128,64]{0,1:T(8,128)S(1)} %psum.63, f32[128]{0:T(128)S(1)} %get-tuple-element.133), kind=kOutput, calls=%fused_computation.311 | convolution fusion | flops 805314560 | bytes 6324736 | tf_op jit(solution)/shard_map/psm,im->psi/dot_general | solution.py:59
  509.9 4.9 fusion.57
  519.7 5.4 collective-permute-start
  548.3 5.2 fusion.409
  583.8 10.3 %fusion.10 = f32[8,16,64,64]{3,2,1,0:T(8,128)S(1)} fusion(f32[16,70,8,64]{3,2,1,0:T(8,128)} %reshape.2901, f32[8,64,70,1]{2,0,1,3:T(8,128)} %get-tuple-element.61), kind=kOutput, calls=%fused_computation.18 | convolution fusion | flops 440401920 | bytes 4534272 | tf_op jit(solution)/shard_map/txi,yitm->yxtm/dot_general | solution.py:130
  594.1 11.8 %fusion.12 = f32[8,16,64,64]{3,2,1,0:T(8,128)} fusion(f32[16,70,8,64]{3,2,1,0:T(8,128)} %reshape.2900, f32[8,64,70,1]{2,0,1,3:T(8,128)S(1)} %copy-done.17), kind=kOutput, calls=%fused_computation.20 | convolution fusion | flops 440401920 | bytes 4534272 | tf_op jit(solution)/shard_map/txi,yitm->yxtm/dot_general | solution.py:130
  606.0 9.4 %fusion.2 = f32[8,16,64,64]{3,2,1,0:T(8,128)} fusion(f32[16,70,8,64]{3,2,1,0:T(8,128)S(1)} %bitcast.856, f32[8,64,70,1]{2,0,1,3:T(8,128)S(1)} %copy-done.16), kind=kOutput, calls=%fused_computation.10 | convolution fusion | flops 440401920 | bytes 4534272 | tf_op jit(solution)/shard_map/txi,yitm->yxtm/dot_general | solution.py:130
  615.4 9.9 %fusion.4 = f32[8,16,64,64]{3,2,1,0:T(8,128)} fusion(f32[16,70,8,64]{3,2,1,0:T(8,128)S(1)} %bitcast.854, f32[8,64,70,1]{2,0,1,3:T(8,128)S(1)} %copy-done.15), kind=kOutput, calls=%fused_computation.12 | convolution fusion | flops 440401920 | bytes 4534272 | tf_op jit(solution)/shard_map/txi,yitm->yxtm/dot_general | solution.py:130
  625.3 9.5 %fusion.6 = f32[8,16,64,64]{3,2,1,0:T(8,128)} fusion(f32[16,70,8,64]{3,2,1,0:T(8,128)S(1)} %bitcast.852, f32[8,64,70,1]{2,0,1,3:T(8,128)S(1)} %copy-done.14), kind=kOutput, calls=%fused_computation.14 | convolution fusion | flops 440401920 | bytes 4534272 | tf_op jit(solution)/shard_map/txi,yitm->yxtm/dot_general | solution.py:130
  634.9 9.4 %fusion.8 = f32[8,16,64,64]{3,2,1,0:T(8,128)} fusion(f32[16,70,8,64]{3,2,1,0:T(8,128)S(1)} %bitcast.850, f32[8,64,70,1]{2,0,1,3:T(8,128)S(1)} %get-tuple-element.60), kind=kOutput, calls=%fused_computation.16 | convolution fusion | flops 440401920 | bytes 4534272 | tf_op jit(solution)/shard_map/txi,yitm->yxtm/dot_general | solution.py:130
  644.3 13.5 %add_bitcast_fusion = f32[16,64,8,64]{1,3,0,2:T(8,128)} fusion(f32[8,16,64,64]{3,2,1,0:T(8,128)S(1)} %copy-done.10, f32[8,16,64,64]{3,2,1,0:T(8,128)} %fusion.4, f32[8,16,64,64]{3,2,1,0:T(8,128)} %fusion.6, f32[8,16,64,64]{3,2,1,0:T(8,128)} %fusion.8, f32[8,16,64,64]{3,2,1,0:T(8,128)S(1)} %copy-done.9, f32[8,16,64,64]{3,2,1,0:T(8,128)S(1)} %fusion.10, ...), kind=kOutput, calls=%fused_computation.24 | convolution fusion | flops 443547648 | bytes 17117184 | tf_op jit(solution)/shard_map/txi,yitm->yxtm/dot_general | solution.py:130
  657.8 5.3 copy.99
  663.2 7.8 %convolution_bitcast_fusion = f32[16,64,8,64]{3,2,1,0:T(8,128)} fusion(f32[16,64,8,64]{3,2,1,0:T(8,128)} %copy.99, f32[8,8]{1,0:T(8,128)S(1)} %copy-done.45), kind=kOutput, calls=%fused_computation.40 | convolution fusion | flops 50331648 | bytes 4194560 | tf_op jit(solution)/shard_map/st,yxtm->yxsm/dot_general | solution.py:136
  (306 shorter events, 151.3 us)
Async XLA Ops:
  0.0 532.9 %copy-start = (f32[8,7,7]{2,0,1:T(8,128)S(1)}, f32[8,7,7]{2,0,1:T(8,128)}, u32[]{:S(2)}) copy-start(f32[8,7,7]{2,0,1:T(8,128)} %param.16) | copy-start | bytes 4708
  0.0 24.1 %copy-start.13 = (f32[16,64,512]{2,1,0:T(8,128)S(1)}, f32[16,64,512]{2,1,0:T(8,128)}, u32[]{:S(2)}) copy-start(f32[16,64,512]{2,1,0:T(8,128)} %param.9) | copy-start | bytes 6291460
  29.4 49.5 %copy-start.8 = (f32[1024,8,64]{0,2,1:T(8,128)}, f32[1024,8,64]{0,2,1:T(8,128)S(1)}, u32[]{:S(2)}) copy-start(f32[1024,8,64]{0,2,1:T(8,128)S(1)} %copy.67) | copy-start | bytes 6291460
  84.0 45.9 %copy-start.46 = (f32[8,128]{1,0:T(8,128)S(1)}, f32[8,128]{1,0:T(8,128)}, u32[]{:S(2)}) copy-start(f32[8,128]{1,0:T(8,128)} %param.12) | copy-start | bytes 12292
  86.8 49.9 %copy-start.47 = (f32[8,128]{1,0:T(8,128)S(1)}, f32[8,128]{1,0:T(8,128)}, u32[]{:S(2)}) copy-start(f32[8,128]{1,0:T(8,128)} %param.13) | copy-start | bytes 12292
  86.8 50.5 %copy-start.22 = (f32[16,128]{1,0:T(8,128)S(1)}, f32[16,128]{1,0:T(8,128)}, u32[]{:S(2)}) copy-start(f32[16,128]{1,0:T(8,128)} %get-tuple-element.135) | copy-start | bytes 24580
  144.4 48.7 %copy-start.2 = (f32[1024,8,64]{0,2,1:T(8,128)S(1)}, f32[1024,8,64]{0,2,1:T(8,128)}, u32[]{:S(2)}) copy-start(f32[1024,8,64]{0,2,1:T(8,128)} %fusion.39) | copy-start | bytes 6291460
  148.6 52.1 %copy-start.21 = (f32[16,128]{1,0:T(8,128)S(1)}, f32[16,128]{1,0:T(8,128)}, u32[]{:S(2)}) copy-start(f32[16,128]{1,0:T(8,128)} %get-tuple-element.136) | copy-start | bytes 24580
  207.7 47.1 %copy-start.3 = (f32[1024,8,64]{0,2,1:T(8,128)S(1)}, f32[1024,8,64]{0,2,1:T(8,128)}, u32[]{:S(2)}) copy-start(f32[1024,8,64]{0,2,1:T(8,128)} %fusion.42) | copy-start | bytes 6291460
  212.1 50.2 %copy-start.20 = (f32[16,128]{1,0:T(8,128)S(1)}, f32[16,128]{1,0:T(8,128)}, u32[]{:S(2)}) copy-start(f32[16,128]{1,0:T(8,128)} %get-tuple-element.137) | copy-start | bytes 24580
  269.3 48.7 %copy-start.4 = (f32[1024,8,64]{0,2,1:T(8,128)S(1)}, f32[1024,8,64]{0,2,1:T(8,128)}, u32[]{:S(2)}) copy-start(f32[1024,8,64]{0,2,1:T(8,128)} %fusion.45) | copy-start | bytes 6291460
  273.5 52.0 %copy-start.19 = (f32[16,128]{1,0:T(8,128)S(1)}, f32[16,128]{1,0:T(8,128)}, u32[]{:S(2)}) copy-start(f32[16,128]{1,0:T(8,128)} %get-tuple-element.138) | copy-start | bytes 24580
  332.5 47.1 %copy-start.5 = (f32[1024,8,64]{0,2,1:T(8,128)S(1)}, f32[1024,8,64]{0,2,1:T(8,128)}, u32[]{:S(2)}) copy-start(f32[1024,8,64]{0,2,1:T(8,128)} %fusion.48) | copy-start | bytes 6291460
  336.9 50.1 %copy-start.18 = (f32[16,128]{1,0:T(8,128)S(1)}, f32[16,128]{1,0:T(8,128)}, u32[]{:S(2)}) copy-start(f32[16,128]{1,0:T(8,128)} %get-tuple-element.139) | copy-start | bytes 24580
  394.1 48.7 %copy-start.6 = (f32[1024,8,64]{0,2,1:T(8,128)S(1)}, f32[1024,8,64]{0,2,1:T(8,128)}, u32[]{:S(2)}) copy-start(f32[1024,8,64]{0,2,1:T(8,128)} %fusion.51) | copy-start | bytes 6291460
  517.2 10.3 %copy-start.12 = (f32[1024,8,64]{0,2,1:T(8,128)S(1)}, f32[1024,8,64]{0,2,1:T(8,128)}, u32[]{:S(2)}) copy-start(f32[1024,8,64]{0,2,1:T(8,128)} %copy-done.11) | copy-start | bytes 6291460
  519.7 14.1 %collective-permute-start = (f32[3,64,512]{2,1,0:T(8,128)}, f32[3,64,512]{2,1,0:T(8,128)}, u32[]{:S(2)}, u32[]{:S(2)}) collective-permute-start(f32[3,64,512]{2,1,0:T(8,128)} %slice.114), channel_id=1, source_target_pairs={{0,8},{8,16},{16,24},{1,9},{9,17},{17,25},{2,10},{10,18},{18,26},{... | collective-permute-start | bytes 1179656 | tf_op jit(solution)/shard_map/ppermute | solution.py:18
  525.6 9.1 %collective-permute-start.1 = (f32[3,64,512]{2,1,0:T(8,128)S(1)}, f32[3,64,512]{2,1,0:T(8,128)S(1)}, u32[]{:S(2)}, u32[]{:S(2)}) collective-permute-start(f32[3,64,512]{2,1,0:T(8,128)S(1)} %slice.116), channel_id=1, source_target_pairs={{8,0},{16,8},{24,16},{9,1},{17,9},{25,17},{10,2},{18,10},{26,18},{... | collective-permute-start | bytes 1179656 | tf_op jit(solution)/shard_map/ppermute | solution.py:19
  535.6 7.4 %collective-permute-start.2 = (f32[22,3,512]{2,1,0:T(4,128)S(1)}, f32[22,3,512]{2,1,0:T(4,128)S(1)}, u32[]{:S(2)}, u32[]{:S(2)}) collective-permute-start(f32[22,3,512]{2,1,0:T(4,128)S(1)} %get-tuple-element.52), channel_id=1, source_target_pairs={{0,1},{1,2},{2,3},{3,4},{4,5},{5,6},{6,7},{8,9},{9,10},{10,11},{11... | collective-permute-start | bytes 405512 | tf_op jit(solution)/shard_map/ppermute | solution.py:18
  538.4 8.3 %collective-permute-start.3 = (f32[22,3,512]{2,1,0:T(4,128)S(1)}, f32[22,3,512]{2,1,0:T(4,128)S(1)}, u32[]{:S(2)}, u32[]{:S(2)}) collective-permute-start(f32[22,3,512]{2,1,0:T(4,128)S(1)} %get-tuple-element.53), channel_id=1, source_target_pairs={{1,0},{2,1},{3,2},{4,3},{5,4},{6,5},{7,6},{9,8},{10,9},{11,10},{12... | collective-permute-start | bytes 405512 | tf_op jit(solution)/shard_map/ppermute | solution.py:19
  581.2 24.8 %slice-start.6 = ((s8[4587520]{0:T(1024)(128)(4,1)}), s8[393216]{0:T(1024)(128)(4,1)S(1)}, s32[]{:S(2)}) async-start(s8[4587520]{0:T(1024)(128)(4,1)} %bitcast.855), calls=%async_computation.6 | async-start | bytes 786432
  583.8 10.3 %copy-start.17 = (f32[8,64,70,1]{2,0,1,3:T(8,128)S(1)}, f32[8,64,70,1]{2,0,1,3:T(8,128)}, u32[]{:S(2)}) copy-start(f32[8,64,70,1]{2,0,1,3:T(8,128)} %get-tuple-element.62) | copy-start | bytes 430084
  583.8 22.2 %slice-start.7 = ((s8[4587520]{0:T(1024)(128)(4,1)}), s8[4194304]{0:T(1024)(128)(4,1)S(1)}, s32[]{:S(2)}) async-start(s8[4587520]{0:T(1024)(128)(4,1)} %bitcast.855), calls=%async_computation.7 | async-start | bytes 8388608
  594.1 11.8 %copy-start.16 = (f32[8,64,70,1]{2,0,1,3:T(8,128)S(1)}, f32[8,64,70,1]{2,0,1,3:T(8,128)}, u32[]{:S(2)}) copy-start(f32[8,64,70,1]{2,0,1,3:T(8,128)} %get-tuple-element.57) | copy-start | bytes 430084
  594.1 21.3 %slice-start.4 = ((s8[4587520]{0:T(1024)(128)(4,1)}), s8[4194304]{0:T(1024)(128)(4,1)S(1)}, s32[]{:S(2)}) async-start(s8[4587520]{0:T(1024)(128)(4,1)} %bitcast.853), calls=%async_computation.4 | async-start | bytes 8388608
  594.1 31.2 %slice-start.2 = ((s8[4587520]{0:T(1024)(128)(4,1)}), s8[4194304]{0:T(1024)(128)(4,1)S(1)}, s32[]{:S(2)}) async-start(s8[4587520]{0:T(1024)(128)(4,1)} %bitcast.851), calls=%async_computation.2 | async-start | bytes 8388608
  606.0 19.3 %slice-start.3 = ((s8[4587520]{0:T(1024)(128)(4,1)}), s8[393216]{0:T(1024)(128)(4,1)S(1)}, s32[]{:S(2)}) async-start(s8[4587520]{0:T(1024)(128)(4,1)} %bitcast.851), calls=%async_computation.3 | async-start | bytes 786432
  615.4 9.9 %copy-start.14 = (f32[8,64,70,1]{2,0,1,3:T(8,128)S(1)}, f32[8,64,70,1]{2,0,1,3:T(8,128)}, u32[]{:S(2)}) copy-start(f32[8,64,70,1]{2,0,1,3:T(8,128)} %get-tuple-element.59) | copy-start | bytes 430084
  615.4 19.4 %slice-start = ((s8[4587520]{0:T(1024)(128)(4,1)}), s8[4194304]{0:T(1024)(128)(4,1)S(1)}, s32[]{:S(2)}) async-start(s8[4587520]{0:T(1024)(128)(4,1)} %bitcast.849), calls=%async_computation | async-start | bytes 8388608
  625.3 9.6 %slice-start.1 = ((s8[4587520]{0:T(1024)(128)(4,1)}), s8[393216]{0:T(1024)(128)(4,1)S(1)}, s32[]{:S(2)}) async-start(s8[4587520]{0:T(1024)(128)(4,1)} %bitcast.849), calls=%async_computation.1 | async-start | bytes 786432
  625.3 19.0 %slice-start.8 = ((s8[4587520]{0:T(1024)(128)(4,1)}), s8[4194304]{0:T(1024)(128)(4,1)S(1)}, s32[]{:S(2)}) async-start(s8[4587520]{0:T(1024)(128)(4,1)} %bitcast.857), calls=%async_computation.8 | async-start | bytes 8388608
  663.2 12.6 %copy-start.1 = (f32[8,7,7]{2,0,1:T(8,128)S(1)}, f32[8,7,7]{2,0,1:T(8,128)}, u32[]{:S(2)}) copy-start(f32[8,7,7]{2,0,1:T(8,128)} %param.16) | copy-start | bytes 4708
  (44 other events, 251.0 us)
where the time goes:
time: 687 us; the launch traced here: 676 us
  blocking collectives  322 us (47%)
  matrix products  179 us (26%)
  local copies, waits for them, and re-layouts  118 us (17%)
  between operations  21.8 us (3%)
  other arithmetic  17 us (2%)
  starting transfers between devices  13.5 us (2%)
    psum x8, blocking collectives, shards(): predicted = lax.psum(partial_value, ('rows', 'cols'))  322 us
    dot_general x7, matrix products, shards(): jnp.einsum('txi,yitm->yxtm', band_matrix[:, vertical], padded_grid[vertic...  73.8 us
    dot_general x8, matrix products, refresh_block(): jnp.einsum('psm,im->psi', members_view, spread, precision=lax.Precision.H...  50.9 us
    dot_general x8, matrix products, refresh_block(): jnp.einsum('psi,im->psm', covariance * taper[:, None, :], kalman_gain, pr...  45.7 us
    slice x8, local copies, waits for them, and re-layouts, shards(): padded_grid[vertical:vertical + tile_height]  35.5 us
    add x7, local copies, waits for them, and re-layouts, refresh_block(): return (members_view + increment).reshape(rows_count, cols_count, channels)  26.4 us
    gather x8, local copies, waits for them, and re-layouts, local_prediction(): ensemble.reshape(tile_height * tile_width, species, members)[flat_index]  23.4 us
  transfers between devices with their start and end apart: 4, of which 3 were waited for; matrix products, arithmetic and copies ran while one was open for 1% of the time, Pallas kernels for 0%

commit v1 on v0

v1 whole, which is shorter than its diff:
```python
import functools

import jax
import jax.numpy as jnp
from jax import lax
from jax.experimental import pallas as pl
from jax.experimental.pallas import tpu as pltpu
from jax.sharding import PartitionSpec as P

BATCHES = 8
OBS = 128
SPECIES = 8
MEMBERS = 64
KW = 7
HALO = KW // 2
HALFW = 48
BF16 = jnp.bfloat16
F32 = jnp.float32
VMEM = pl.BlockSpec(memory_space=pltpu.VMEM)
SMEM = pl.BlockSpec(memory_space=pltpu.SMEM)
PARAMS = pltpu.CompilerParams(vmem_limit_bytes=56 << 20)


def split(x):
    high = x.astype(BF16)
    return high, (x - high.astype(F32)).astype(BF16)


def dot(a, b):
    return jnp.dot(a, b, preferred_element_type=F32)


def swap_halves(x):
    return pltpu.roll(x, MEMBERS, axis=x.ndim - 1)


def low_lanes(shape):
    return lax.broadcasted_iota(jnp.int32, shape, len(shape) - 1) < MEMBERS


def taper_weights(squared):
    inverse = lax.rsqrt(jnp.maximum(squared, 1.0))
    ratio = squared * inverse * (1.0 / HALFW)
    outer_inverse = (2.0 * HALFW / 3.0) * inverse
    inner = (((-0.25 * ratio + 0.5) * ratio + 0.625) * ratio - 5.0 / 3.0) * ratio * ratio + 1.0
    outer = (
        ((((ratio * (1.0 / 12.0) - 0.5) * ratio + 0.625) * ratio + 5.0 / 3.0) * ratio - 5.0) * ratio
        + 4.0
        - outer_inverse
    )
    return jnp.where(ratio <= 1.0, inner, jnp.where(ratio < 2.0, outer, 0.0))


def place(cols_count):
    return lax.axis_index("rows"), lax.axis_index("cols")


def gather_kernel(width, order, cells, weight_ref, prior_ref, out_ref, picked):
    height, cols = prior_ref.shape[0], prior_ref.shape[1]
    my_row, my_col = lax.axis_index("rows"), lax.axis_index("cols")
    mine = 2 * lax.rem(my_row, 2) + lax.rem(lax.div(my_row, 2), 2)
    out_ref[...] = jnp.zeros_like(out_ref)
    for k in range(BATCHES):
        batch = order[k]
        first = cells[batch, 0]
        owner = (lax.div(first, width * height) == my_row) & (
            lax.div(lax.rem(first, width), cols) == my_col
        )

        @pl.when(owner)
        def _():
            def one(i, carry):
                cell = cells[batch, i]
                row = lax.div(cell, width) - my_row * height
                col = lax.rem(cell, width) - my_col * cols
                picked[pl.ds(i, 1), :] = prior_ref[row, pl.ds(col, 1), :]
                return carry

            lax.fori_loop(0, OBS, one, 0, unroll=8)
            weights = weight_ref[batch]
            low = low_lanes((OBS, 2 * MEMBERS))
            total = jnp.zeros((OBS, 2 * MEMBERS), F32)
            for p in range(SPECIES // 2):
                scale = jnp.where(low, weights[:, 2 * p : 2 * p + 1], weights[:, 2 * p + 1 : 2 * p + 2])
                total = total + scale * picked[:, 128 * p : 128 * (p + 1)]
            total = total + swap_halves(total)
            slot = jnp.bitwise_xor(k % 4, mine)
            keep = low if k < 4 else jnp.logical_not(low)
            out_ref[slot] = jnp.where(keep, total, out_ref[slot])


def exchange(parts):
    size = lax.axis_size("rows")
    cols = lax.axis_size("cols")

    def rows(x, bit):
        return lax.ppermute(x, "rows", [(i, i ^ bit) for i in range(size)])

    kept = parts[:2] + rows(parts[2:], 1)
    kept = kept[0] + rows(kept[1], 2)
    bit = 4
    while bit < size:
        kept = kept + rows(kept, bit)
        bit *= 2
    bit = 1
    while bit < cols:
        kept = kept + lax.ppermute(kept, "cols", [(i, i ^ bit) for i in range(cols)])
        bit *= 2
    other = rows(kept, 2)
    return kept, other, rows(kept, 1), rows(other, 1)


def main_kernel(
    width, order, cells, mask, cell_ref, value_ref, var_ref, prior_ref, p0, p1, p2, p3,
    out_ref, left_ref, right_ref, predicted, table,
):
    height, cols = prior_ref.shape[0], prior_ref.shape[1]
    my_row, my_col = lax.axis_index("rows"), lax.axis_index("cols")
    across = width // cols
    my_tile = my_row * across + my_col
    mine = 2 * lax.rem(my_row, 2) + lax.rem(lax.div(my_row, 2), 2)
    for rel, part in enumerate((p0, p1, p2, p3)):
        predicted[jnp.bitwise_xor(rel, mine)] = part[...]
    low = low_lanes((cols, 2 * MEMBERS))
    for j in range(height // 2):
        for p in range(SPECIES // 2):
            a = prior_ref[2 * j, :, 128 * p : 128 * (p + 1)]
            b = prior_ref[2 * j + 1, :, 128 * p : 128 * (p + 1)]
            out_ref[j, 2 * p * cols : (2 * p + 1) * cols] = jnp.where(low, a, swap_halves(b))
            out_ref[j, (2 * p + 1) * cols : (2 * p + 2) * cols] = jnp.where(low, swap_halves(a), b)
    batches = [order[k] for k in range(BATCHES)]
    tiles = []
    for k in range(BATCHES):
        first = cells[batches[k], 0]
        tiles.append(lax.div(first, width * height) * across + lax.div(lax.rem(first, width), cols))
        table[k : k + 1, :] = cell_ref[pl.ds(batches[k], 1), :].astype(F32)
        table[8 + k : 9 + k, :] = value_ref[pl.ds(batches[k], 1), :]
        table[16 + k : 17 + k, :] = var_ref[pl.ds(batches[k], 1), :]
    cell_lane = table[0:8, :]
    row_lane = jnp.floor(cell_lane * (1.0 / width))
    col_lane = cell_lane - row_lane * width
    row_col = jnp.transpose(row_lane)
    col_col = jnp.transpose(col_lane)
    value_col = jnp.transpose(table[8:16, :])
    var_col = jnp.transpose(table[16:24, :])
    low_obs = low_lanes((OBS, 2 * MEMBERS))
    x_pos = (my_col * cols + lax.broadcasted_iota(jnp.int32, (cols, OBS), 0)).astype(F32)

    def update(x, taper, spread_w, spread_lo, gain_w, gain_hi):
        high, low_part = split(x)
        cov = dot(jnp.concatenate([high, low_part], 1), spread_w) + dot(high, spread_lo)
        c_high, c_low = split(cov * taper)
        both = dot(c_high, gain_w)
        return x + (both[:, : 2 * MEMBERS] + both[:, 2 * MEMBERS :] + dot(c_low, gain_hi))

    for k in range(BATCHES):
        block = predicted[k % 4]
        if k < 4:
            here = jnp.where(low_obs, block, swap_halves(block))
        else:
            here = jnp.where(low_obs, swap_halves(block), block)
        mean = jnp.sum(here, axis=1, keepdims=True) * (0.5 / MEMBERS)
        spread = here - mean
        variance = jnp.sum(spread * spread, axis=1, keepdims=True) * (0.5 / (MEMBERS - 1))
        var = var_col[:, k : k + 1]
        denominator = variance + var
        shrink = 1.0 / (1.0 + jnp.sqrt(var / denominator))
        gain = ((value_col[:, k : k + 1] - mean) - shrink * spread) / (
            denominator * (MEMBERS - 1)
        )
        turned = jnp.transpose(spread)
        top = lax.broadcasted_iota(jnp.int32, turned.shape, 0) < MEMBERS
        zero = jnp.zeros_like(turned)
        wide = jnp.concatenate([jnp.where(top, turned, zero), jnp.where(top, zero, turned)], 1)
        wide_hi, wide_lo = split(wide)
        spread_w = jnp.concatenate([wide_hi, wide_hi], 0)
        tall = jnp.concatenate([jnp.where(low_obs, gain, zero), jnp.where(low_obs, zero, gain)], 0)
        tall_hi, tall_lo = split(tall)
        gain_w = jnp.concatenate([tall_hi, tall_lo], 1)
        obs_row, obs_col = row_lane[k : k + 1, :], col_lane[k : k + 1, :]
        if k < BATCHES - 1:
            for q in range(4):
                if q + 4 <= k:
                    continue
                halves = []
                for later in (q, q + 4):
                    dr = row_col[:, later : later + 1] - obs_row
                    dc = col_col[:, later : later + 1] - obs_col
                    active = (mask[batches[k], tiles[later]] > 0).astype(F32)
                    halves.append(taper_weights(dr * dr + dc * dc) * active)
                predicted[q] = update(
                    predicted[q], jnp.concatenate(halves, 1), spread_w, wide_lo, gain_w, tall_hi
                )

        @pl.when(mask[batches[k], my_tile] > 0)
        def _():
            dx = x_pos - obs_col
            dx = dx * dx

            def pair(j, carry):
                halves = []
                for h in range(2):
                    dy = (my_row * height + 2 * j + h).astype(F32) - obs_row
                    halves.append(taper_weights(dx + dy * dy))
                taper = jnp.concatenate(halves, 1)
                taper = jnp.concatenate([taper] * SPECIES, 0)
                out_ref[j] = update(out_ref[j], taper, spread_w, wide_lo, gain_w, tall_hi)
                return carry

            lax.fori_loop(0, height // 2, pair, 0)

    for j in range(height // 2):
        for e in range(HALO):
            for t in range(SPECIES):
                left_ref[j, e, t : t + 1, :] = out_ref[j, t * cols + e : t * cols + e + 1, :]
                r = t * cols + cols - HALO + e
                right_ref[j, e, t : t + 1, :] = out_ref[j, r : r + 1, :]


def smooth_kernel(kern, mix, tile_ref, left_ref, right_ref, up_ref, down_ref, out_ref, padded, lines):
    pairs, cols = tile_ref.shape[0], tile_ref.shape[1] // SPECIES
    depth = cols + 16
    lanes = 2 * MEMBERS
    half = 3 * SPECIES
    edge = jnp.zeros((8, lanes), F32)
    for q in range(pairs + 4):
        for t in range(SPECIES):
            padded[q, t, 0:8, :] = edge
            padded[q, t, depth - 8 : depth, :] = edge
            if q < 2:
                body = up_ref[q, t * cols : (t + 1) * cols, :]
            elif q < pairs + 2:
                body = tile_ref[q - 2, t * cols : (t + 1) * cols, :]
            else:
                body = down_ref[q - pairs - 2, t * cols : (t + 1) * cols, :]
            padded[q, t, 8 : 8 + cols, :] = body
            for e in range(HALO):
                at = e * SPECIES + t
                base = SPECIES * cols
                if q < 2:
                    a = up_ref[q, base + at : base + at + 1, :]
                    b = up_ref[q, base + half + at : base + half + at + 1, :]
                elif q < pairs + 2:
                    a = left_ref[q - 2, e, t : t + 1, :]
                    b = right_ref[q - 2, e, t : t + 1, :]
                else:
                    a = down_ref[q - pairs - 2, base + at : base + at + 1, :]
                    b = down_ref[q - pairs - 2, base + half + at : base + half + at + 1, :]
                padded[q, t, 5 + e : 6 + e, :] = a
                padded[q, t, 8 + cols + e : 9 + cols + e, :] = b
    offset = lax.broadcasted_iota(jnp.int32, (cols, depth), 1) - (
        lax.broadcasted_iota(jnp.int32, (cols, depth), 0) + 5
    )
    low = low_lanes((cols, lanes))

    def species(t, carry):
        bands = []
        for a in range(KW):
            band = jnp.zeros((cols, depth), F32)
            for e in range(KW):
                band = jnp.where(offset == e, kern[t, a * KW + e], band)
            bands.append(band)
        band_hi, band_lo = split(jnp.concatenate(bands, 0))
        for d in range(0, pairs + 4, 2):
            data = jnp.concatenate([padded[d, t], padded[d + 1, t]], 1)
            hi, lo = split(data)
            product = dot(band_hi, hi) + dot(band_hi, lo) + dot(band_lo, hi)
            lines[d] = product[:, :lanes]
            lines[d + 1] = product[:, lanes:]

        def part(q, a):
            return lines[q, a * cols : (a + 1) * cols, :]

        def odd(u):
            return swap_halves(part(u, 0) + part(u + 1, 2) + part(u + 2, 4) + part(u + 3, 6))

        before = odd(0)
        for j in range(pairs):
            after = odd(j + 1)
            straight = part(j + 1, 1) + part(j + 2, 3) + part(j + 3, 5)
            padded[j, t, 0:cols, :] = straight + jnp.where(low, before, after)
            before = after
        return carry

    lax.fori_loop(0, SPECIES, species, 0)

    def mixed(j, carry):
        smooth = [padded[j, t, 0:cols, :] for t in range(SPECIES)]
        for p in range(SPECIES // 2):
            total = []
            for s in (2 * p, 2 * p + 1):
                acc = mix[s, 0] * smooth[0]
                for t in range(1, SPECIES):
                    acc = acc + mix[s, t] * smooth[t]
                total.append(acc)
            out_ref[2 * j, :, 128 * p : 128 * (p + 1)] = jnp.where(low, total[0], swap_halves(total[1]))
            out_ref[2 * j + 1, :, 128 * p : 128 * (p + 1)] = jnp.where(
                low, swap_halves(total[0]), total[1]
            )
        return carry

    lax.fori_loop(0, pairs, mixed, 0)


def shards(prior, obs_cell, obs_weight, obs_value, obs_var, loc_mask, batch_order, kernel, mixing):
    height, cols, channels = prior.shape
    across = lax.axis_size("cols")
    width = cols * across
    pairs = height // 2
    lanes = 2 * MEMBERS
    parts = pl.pallas_call(
        functools.partial(gather_kernel, width),
        out_shape=jax.ShapeDtypeStruct((4, OBS, lanes), F32),
        in_specs=[SMEM, SMEM, VMEM, VMEM],
        out_specs=VMEM,
        scratch_shapes=[pltpu.VMEM((OBS, channels), F32)],
        compiler_params=PARAMS,
        name="gather",
    )(batch_order, obs_cell, obs_weight, prior)
    arrived = exchange(parts)
    tile, left, right = pl.pallas_call(
        functools.partial(main_kernel, width),
        out_shape=(
            jax.ShapeDtypeStruct((pairs, SPECIES * cols, lanes), F32),
            jax.ShapeDtypeStruct((pairs, HALO, SPECIES, lanes), F32),
            jax.ShapeDtypeStruct((pairs, HALO, SPECIES, lanes), F32),
        ),
        in_specs=[SMEM] * 3 + [VMEM] * 8,
        out_specs=(VMEM, VMEM, VMEM),
        scratch_shapes=[pltpu.VMEM((4, OBS, lanes), F32), pltpu.VMEM((24, OBS), F32)],
        compiler_params=PARAMS,
        name="assimilate",
    )(batch_order, obs_cell, loc_mask, obs_cell, obs_value, obs_var, prior, *arrived)

    def shift(x, axis, step):
        size = lax.axis_size(axis)
        return lax.ppermute(
            x, axis, [(i, i + step) for i in range(size) if 0 <= i + step < size]
        )

    from_left = shift(right, "cols", 1)
    from_right = shift(left, "cols", -1)

    def with_sides(lo, hi):
        flat = (hi - lo, HALO * SPECIES, lanes)
        return jnp.concatenate(
            [tile[lo:hi], from_left[lo:hi].reshape(flat), from_right[lo:hi].reshape(flat)], 1
        )

    above = shift(with_sides(pairs - 2, pairs), "rows", 1)
    below = shift(with_sides(0, 2), "rows", -1)
    return pl.pallas_call(
        smooth_kernel,
        out_shape=jax.ShapeDtypeStruct((height, cols, channels), F32),
        in_specs=[SMEM, SMEM] + [VMEM] * 5,
        out_specs=VMEM,
        scratch_shapes=[
            pltpu.VMEM((pairs + 4, SPECIES, cols + 16, lanes), F32),
            pltpu.VMEM((pairs + 4, KW * cols, lanes), F32),
        ],
        compiler_params=PARAMS,
        name="smooth",
    )(kernel.reshape(SPECIES, KW * KW), mixing, tile, from_left, from_right, above, below)


def solution(mesh):
    return jax.shard_map(
        shards,
        mesh=mesh,
        in_specs=(P("rows", "cols", None), P(), P(), P(), P(), P(), P(), P(), P()),
        out_specs=P("rows", "cols", None),
        check_vma=False,
    )
```

time: 687 us -> 132 us (0.19)
  the two profiles are of different devices: /device:TPU:9 before, /device:TPU:11 now
where the time goes in v1:
time: 132 us; the launch traced here: 131 us
  Pallas kernels  58.7 us (44%)
  waiting for transfers between devices  32.9 us (25%)
  starting transfers between devices  32.5 us (25%)
  local copies, waits for them, and re-layouts  6.1 us (5%)
    pallas_call x1, Pallas kernels, shards(): pl.pallas_call(functools.partial(main_kernel, width), out_shape=(jax.Shap...  40 us
    ppermute x4, waiting for transfers between devices, shift(): lax.ppermute(x, axis, [(i, i + step) for i in range(size) if 0 <= i + ste...  21.1 us
    ppermute x4, starting transfers between devices, shift(): lax.ppermute(x, axis, [(i, i + step) for i in range(size) if 0 <= i + ste...  18.1 us
    pallas_call x1, Pallas kernels, shards(): pl.pallas_call(smooth_kernel, out_shape=jax.ShapeDtypeStruct((height, col...  16 us
    ppermute x5, starting transfers between devices, rows(): return lax.ppermute(x, 'rows', [(i, i ^ bit) for i in range(size)])  9.78 us
    ppermute x3, waiting for transfers between devices, exchange(): lax.ppermute(kept, 'cols', [(i, i ^ bit) for i in range(cols)])  7.97 us
    ppermute x3, starting transfers between devices, exchange(): lax.ppermute(kept, 'cols', [(i, i ^ bit) for i in range(cols)])  4.58 us
    ppermute x5, waiting for transfers between devices, rows(): return lax.ppermute(x, 'rows', [(i, i ^ bit) for i in range(size)])  3.76 us
  transfers between devices with their start and end apart: 12, of which 9 were waited for; matrix products, arithmetic and copies ran while one was open for 2% of the time, Pallas kernels for 0%

profile of v1, /device:TPU:11, one launch (start us, length us, event | category | flops | bytes accessed | tf_op | source)
XLA Modules:
  0.0 131.4 jit_solution(12241900943909835064)
XLA Ops:
  0.0 1.8 %copy.13.weight_ref = f32[8,128,8]{2,1,0:T(8,128)} copy(f32[8,128,8]{1,2,0:T(8,128)} %param.11) | data formatting | bytes 65536 | tf_op args[2]
  1.8 2.6 %gather.1 = f32[4,128,128]{2,1,0:T(8,128)} custom-call(s32[8]{0:T(128)} %order.3, s32[8,128]{1,0:T(8,128)} %cell_ref.1, f32[8,128,8]{2,1,0:T(8,128)} %copy.13.weight_ref, f32[16,64,512]{2,1,0:T(8,128)} %prior_ref.3), custom_call_target="tpu_custom_call" | custom-call | tf_op jit(solution)/shard_map/gather/pallas_call | solution.py:311
  4.4 0.9 slice.41
  5.3 0.7 collective-permute-start
  6.1 1.0 collective-permute-done
  7.0 0.9 slice_add_fusion
  8.0 1.3 collective-permute-start.1
  9.3 1.9 %collective-permute-done.1 = f32[128,128]{1,0:T(8,128)S(1)} collective-permute-done((f32[128,128]{1,0:T(8,128)S(1)}, f32[128,128]{1,0:T(8,128)S(1)}, u32[]{:S(2)}, u32[]{:S(2)}) %collective-permute-start.1) | collective-permute-done | bytes 65568 | tf_op jit(solution)/shard_map/ppermute | solution.py:97
  11.2 0.3 collective-permute-start.2
  11.5 2.9 %collective-permute-done.2 = f32[128,128]{1,0:T(8,128)S(1)} collective-permute-done((f32[128,128]{1,0:T(8,128)S(1)}, f32[128,128]{1,0:T(8,128)S(1)}, u32[]{:S(2)}, u32[]{:S(2)}) %collective-permute-start.2) | collective-permute-done | bytes 65568 | tf_op jit(solution)/shard_map/ppermute | solution.py:107
  14.4 0.2 collective-permute-start.3
  14.6 2.9 %collective-permute-done.3 = f32[128,128]{1,0:T(8,128)S(1)} collective-permute-done((f32[128,128]{1,0:T(8,128)S(1)}, f32[128,128]{1,0:T(8,128)S(1)}, u32[]{:S(2)}, u32[]{:S(2)}) %collective-permute-start.3) | collective-permute-done | bytes 65568 | tf_op jit(solution)/shard_map/ppermute | solution.py:107
  17.6 4.0 %collective-permute-start.4 = (f32[128,128]{1,0:T(8,128)S(1)}, f32[128,128]{1,0:T(8,128)S(1)}, u32[]{:S(2)}, u32[]{:S(2)}) collective-permute-start(f32[128,128]{1,0:T(8,128)S(1)} %add.18), channel_id=1, source_target_pairs={{0,4},{1,5},{2,6},{3,7},{4,0},{5,1},{6,2},{7,3},{8,12},{9,13},{10,... | collective-permute-start | bytes 196616 | tf_op jit(solution)/shard_map/ppermute | solution.py:107
  21.6 2.2 %collective-permute-done.4 = f32[128,128]{1,0:T(8,128)S(1)} collective-permute-done((f32[128,128]{1,0:T(8,128)S(1)}, f32[128,128]{1,0:T(8,128)S(1)}, u32[]{:S(2)}, u32[]{:S(2)}) %collective-permute-start.4) | collective-permute-done | bytes 65568 | tf_op jit(solution)/shard_map/ppermute | solution.py:107
  23.8 0.1 collective-permute-start.5
  23.9 4.4 %collective-permute-start.6 = (f32[128,128]{1,0:T(8,128)S(1)}, f32[128,128]{1,0:T(8,128)S(1)}, u32[]{:S(2)}, u32[]{:S(2)}) collective-permute-start(f32[128,128]{1,0:T(8,128)S(1)} %add.19.p0), channel_id=1, source_target_pairs={{0,8},{8,0},{16,24},{24,16},{1,9},{9,1},{17,25},{25,17},{2,10},{10... | collective-permute-start | bytes 196616 | tf_op jit(solution)/shard_map/ppermute | solution.py:97
  28.3 3.2 %collective-permute-start.7 = (f32[128,128]{1,0:T(8,128)S(1)}, f32[128,128]{1,0:T(8,128)S(1)}, u32[]{:S(2)}, u32[]{:S(2)}) collective-permute-start(f32[128,128]{1,0:T(8,128)S(1)} %collective-permute-done.5.p1), channel_id=1, source_target_pairs={{0,8},{8,0},{16,24},{24,16},{1,9},{9,1},{17,25},{25,17},{2,10},{10... | collective-permute-start | bytes 196616 | tf_op jit(solution)/shard_map/ppermute | solution.py:97
  31.5 0.9 collective-permute-done.7.p3
  32.4 0.6 copy-done.7
  33.1 40.0 %assimilate.1 = (f32[8,512,128]{2,1,0:T(8,128)}, f32[8,3,8,128]{3,2,1,0:T(8,128)}, f32[8,3,8,128]{3,2,1,0:T(8,128)}) custom-call(s32[8]{0:T(128)} %order.3, s32[8,128]{1,0:T(8,128)} %cell_ref.1, s32[8,32]{1,0:T(8,128)} %mask.1, s32[8,128]{1,0:T(8,128)} %cell_ref.1, f32[8,128]{1,0:T(8,128)} %value_ref.1, f32[8,128]{1,0:T(8,128)} %var_ref.1, ...), custom_call_target="tpu_custom_call" | custom-call | tf_op jit(solution)/shard_map/assimilate/pallas_call | solution.py:321
  73.1 10.8 %collective-permute-start.8 = (f32[8,3,8,128]{3,2,1,0:T(8,128)}, f32[8,3,8,128]{3,2,1,0:T(8,128)S(1)}, u32[]{:S(2)}, u32[]{:S(2)}) collective-permute-start(f32[8,3,8,128]{3,2,1,0:T(8,128)} %get-tuple-element.9), channel_id=1, source_target_pairs={{0,1},{1,2},{2,3},{3,4},{4,5},{5,6},{6,7},{8,9},{9,10},{10,11},{11... | collective-permute-start | bytes 294920 | tf_op jit(solution)/shard_map/ppermute | solution.py:337
  83.9 1.9 %collective-permute-start.9 = (f32[8,3,8,128]{3,2,1,0:T(8,128)}, f32[8,3,8,128]{3,2,1,0:T(8,128)S(1)}, u32[]{:S(2)}, u32[]{:S(2)}) collective-permute-start(f32[8,3,8,128]{3,2,1,0:T(8,128)} %get-tuple-element.10), channel_id=1, source_target_pairs={{1,0},{2,1},{3,2},{4,3},{5,4},{6,5},{7,6},{9,8},{10,9},{11,10},{12... | collective-permute-start | bytes 294920 | tf_op jit(solution)/shard_map/ppermute | solution.py:337
  85.9 0.0 copy-start.8
  85.9 1.3 fusion.1
  87.2 12.7 %collective-permute-done.9.right_ref = f32[8,3,8,128]{3,2,1,0:T(8,128)S(1)} collective-permute-done((f32[8,3,8,128]{3,2,1,0:T(8,128)}, f32[8,3,8,128]{3,2,1,0:T(8,128)S(1)}, u32[]{:S(2)}, u32[]{:S(2)}) %collective-permute-start.9) | collective-permute-done | bytes 98336 | tf_op jit(solution)/shard_map/ppermute | solution.py:337
  100.0 3.5 %collective-permute-start.10 = (f32[2,560,128]{2,1,0:T(8,128)S(1)}, f32[2,560,128]{2,1,0:T(8,128)S(1)}, u32[]{:S(2)}, u32[]{:S(2)}) collective-permute-start(f32[2,560,128]{2,1,0:T(8,128)S(1)} %pad_maximum_fusion), channel_id=1, source_target_pairs={{0,8},{8,16},{16,24},{1,9},{9,17},{17,25},{2,10},{10,18},{18,26},{... | collective-permute-start | bytes 1720328 | tf_op jit(solution)/shard_map/ppermute | solution.py:337
  103.5 1.9 %collective-permute-start.11 = (f32[2,560,128]{2,1,0:T(8,128)S(1)}, f32[2,560,128]{2,1,0:T(8,128)S(1)}, u32[]{:S(2)}, u32[]{:S(2)}) collective-permute-start(f32[2,560,128]{2,1,0:T(8,128)S(1)} %pad_maximum_fusion.1), channel_id=1, source_target_pairs={{8,0},{16,8},{24,16},{9,1},{17,9},{25,17},{10,2},{18,10},{26,18},{... | collective-permute-start | bytes 1720328 | tf_op jit(solution)/shard_map/ppermute | solution.py:337
  105.4 0.7 reshape.15.kern
  106.1 4.0 %collective-permute-done.10.up_ref = f32[2,560,128]{2,1,0:T(8,128)S(1)} collective-permute-done((f32[2,560,128]{2,1,0:T(8,128)S(1)}, f32[2,560,128]{2,1,0:T(8,128)S(1)}, u32[]{:S(2)}, u32[]{:S(2)}) %collective-permute-start.10) | collective-permute-done | bytes 573472 | tf_op jit(solution)/shard_map/ppermute | solution.py:337
  110.1 4.4 %collective-permute-done.11.down_ref = f32[2,560,128]{2,1,0:T(8,128)S(1)} collective-permute-done((f32[2,560,128]{2,1,0:T(8,128)S(1)}, f32[2,560,128]{2,1,0:T(8,128)S(1)}, u32[]{:S(2)}, u32[]{:S(2)}) %collective-permute-start.11) | collective-permute-done | bytes 573472 | tf_op jit(solution)/shard_map/ppermute | solution.py:337
  114.5 0.8 copy-done.1
  115.3 16.0 %smooth.1 = f32[16,64,512]{2,1,0:T(8,128)} custom-call(f32[8,49]{1,0:T(8,128)} %reshape.15.kern, f32[8,8]{1,0:T(8,128)} %mix.1, f32[8,512,128]{2,1,0:T(8,128)} %get-tuple-element.8.tile_ref, f32[8,3,8,128]{3,2,1,0:T(8,128)} %copy-done.3, f32[8,3,8,128]{3,2,1,0:T(8,128)} %copy-done.4, f32[2,560,128]{2,1,0:T(8,128)} %copy-done, f32[2,560,128]{2,1,0:T(8,128)} %copy-done.1), custom_call_target="tpu_custom_call" | custom-call | tf_op jit(solution)/shard_map/smooth/pallas_call | solution.py:352
  (28 shorter events, 0.2 us)
Async XLA Ops:
  5.3 1.7 %collective-permute-start = (f32[2,128,128]{2,1,0:T(8,128)S(1)}, f32[2,128,128]{2,1,0:T(8,128)S(1)}, u32[]{:S(2)}, u32[]{:S(2)}) collective-permute-start(f32[2,128,128]{2,1,0:T(8,128)S(1)} %slice.41), channel_id=1, source_target_pairs={{0,8},{8,0},{16,24},{24,16},{1,9},{9,1},{17,25},{25,17},{2,10},{10... | collective-permute-start | bytes 393224 | tf_op jit(solution)/shard_map/ppermute | solution.py:97
  8.0 3.2 %collective-permute-start.1 = (f32[128,128]{1,0:T(8,128)S(1)}, f32[128,128]{1,0:T(8,128)S(1)}, u32[]{:S(2)}, u32[]{:S(2)}) collective-permute-start(f32[128,128]{1,0:T(8,128)S(1)} %slice_bitcast_fusion), channel_id=1, source_target_pairs={{0,16},{8,24},{16,0},{24,8},{1,17},{9,25},{17,1},{25,9},{2,18},{10... | collective-permute-start | bytes 196616 | tf_op jit(solution)/shard_map/ppermute | solution.py:97
  11.2 3.2 %collective-permute-start.2 = (f32[128,128]{1,0:T(8,128)S(1)}, f32[128,128]{1,0:T(8,128)S(1)}, u32[]{:S(2)}, u32[]{:S(2)}) collective-permute-start(f32[128,128]{1,0:T(8,128)S(1)} %fusion), channel_id=1, source_target_pairs={{0,1},{1,0},{2,3},{3,2},{4,5},{5,4},{6,7},{7,6},{8,9},{9,8},{10,11... | collective-permute-start | bytes 196616 | tf_op jit(solution)/shard_map/ppermute | solution.py:107
  14.4 3.2 %collective-permute-start.3 = (f32[128,128]{1,0:T(8,128)S(1)}, f32[128,128]{1,0:T(8,128)S(1)}, u32[]{:S(2)}, u32[]{:S(2)}) collective-permute-start(f32[128,128]{1,0:T(8,128)S(1)} %add.17), channel_id=1, source_target_pairs={{0,2},{1,3},{2,0},{3,1},{4,6},{5,7},{6,4},{7,5},{8,10},{9,11},{10,... | collective-permute-start | bytes 196616 | tf_op jit(solution)/shard_map/ppermute | solution.py:107
  17.6 6.2 %collective-permute-start.4 = (f32[128,128]{1,0:T(8,128)S(1)}, f32[128,128]{1,0:T(8,128)S(1)}, u32[]{:S(2)}, u32[]{:S(2)}) collective-permute-start(f32[128,128]{1,0:T(8,128)S(1)} %add.18), channel_id=1, source_target_pairs={{0,4},{1,5},{2,6},{3,7},{4,0},{5,1},{6,2},{7,3},{8,12},{9,13},{10,... | collective-permute-start | bytes 196616 | tf_op jit(solution)/shard_map/ppermute | solution.py:107
  23.8 8.7 %copy-start.2 = (f32[128,128]{1,0:T(8,128)}, f32[128,128]{1,0:T(8,128)S(1)}, u32[]{:S(2)}) copy-start(f32[128,128]{1,0:T(8,128)S(1)} %add.19.p0) | copy-start | bytes 196612
  23.8 4.5 %collective-permute-start.5 = (f32[128,128]{1,0:T(8,128)S(1)}, f32[128,128]{1,0:T(8,128)S(1)}, u32[]{:S(2)}, u32[]{:S(2)}) collective-permute-start(f32[128,128]{1,0:T(8,128)S(1)} %add.19.p0), channel_id=1, source_target_pairs={{0,16},{8,24},{16,0},{24,8},{1,17},{9,25},{17,1},{25,9},{2,18},{10... | collective-permute-start | bytes 196616 | tf_op jit(solution)/shard_map/ppermute | solution.py:97
  23.9 7.7 %collective-permute-start.6 = (f32[128,128]{1,0:T(8,128)S(1)}, f32[128,128]{1,0:T(8,128)S(1)}, u32[]{:S(2)}, u32[]{:S(2)}) collective-permute-start(f32[128,128]{1,0:T(8,128)S(1)} %add.19.p0), channel_id=1, source_target_pairs={{0,8},{8,0},{16,24},{24,16},{1,9},{9,1},{17,25},{25,17},{2,10},{10... | collective-permute-start | bytes 196616 | tf_op jit(solution)/shard_map/ppermute | solution.py:97
  28.3 4.2 %copy-start.5 = (f32[128,128]{1,0:T(8,128)}, f32[128,128]{1,0:T(8,128)S(1)}, u32[]{:S(2)}) copy-start(f32[128,128]{1,0:T(8,128)S(1)} %collective-permute-done.5.p1) | copy-start | bytes 196612
  28.3 4.1 %collective-permute-start.7 = (f32[128,128]{1,0:T(8,128)S(1)}, f32[128,128]{1,0:T(8,128)S(1)}, u32[]{:S(2)}, u32[]{:S(2)}) collective-permute-start(f32[128,128]{1,0:T(8,128)S(1)} %collective-permute-done.5.p1), channel_id=1, source_target_pairs={{0,8},{8,0},{16,24},{24,16},{1,9},{9,1},{17,25},{25,17},{2,10},{10... | collective-permute-start | bytes 196616 | tf_op jit(solution)/shard_map/ppermute | solution.py:97
  31.5 0.9 copy-start.6
  32.4 0.6 copy-start.7
  73.1 14.0 %collective-permute-start.8 = (f32[8,3,8,128]{3,2,1,0:T(8,128)}, f32[8,3,8,128]{3,2,1,0:T(8,128)S(1)}, u32[]{:S(2)}, u32[]{:S(2)}) collective-permute-start(f32[8,3,8,128]{3,2,1,0:T(8,128)} %get-tuple-element.9), channel_id=1, source_target_pairs={{0,1},{1,2},{2,3},{3,4},{4,5},{5,6},{6,7},{8,9},{9,10},{10,11},{11... | collective-permute-start | bytes 294920 | tf_op jit(solution)/shard_map/ppermute | solution.py:337
  83.9 16.0 %collective-permute-start.9 = (f32[8,3,8,128]{3,2,1,0:T(8,128)}, f32[8,3,8,128]{3,2,1,0:T(8,128)S(1)}, u32[]{:S(2)}, u32[]{:S(2)}) collective-permute-start(f32[8,3,8,128]{3,2,1,0:T(8,128)} %get-tuple-element.10), channel_id=1, source_target_pairs={{1,0},{2,1},{3,2},{4,3},{5,4},{6,5},{7,6},{9,8},{10,9},{11,10},{12... | collective-permute-start | bytes 294920 | tf_op jit(solution)/shard_map/ppermute | solution.py:337
  85.9 19.6 %copy-start.8 = (f32[8,7,7]{2,0,1:T(8,128)S(1)}, f32[8,7,7]{2,0,1:T(8,128)}, u32[]{:S(2)}) copy-start(f32[8,7,7]{2,0,1:T(8,128)} %param.16) | copy-start | bytes 4708
  87.2 27.4 %copy-start.3 = (f32[8,3,8,128]{3,2,1,0:T(8,128)}, f32[8,3,8,128]{3,2,1,0:T(8,128)S(1)}, u32[]{:S(2)}) copy-start(f32[8,3,8,128]{3,2,1,0:T(8,128)S(1)} %collective-permute-done.8.left_ref) | copy-start | bytes 294916
  99.9 14.6 %copy-start.4 = (f32[8,3,8,128]{3,2,1,0:T(8,128)}, f32[8,3,8,128]{3,2,1,0:T(8,128)S(1)}, u32[]{:S(2)}) copy-start(f32[8,3,8,128]{3,2,1,0:T(8,128)S(1)} %collective-permute-done.9.right_ref) | copy-start | bytes 294916
  100.0 10.1 %collective-permute-start.10 = (f32[2,560,128]{2,1,0:T(8,128)S(1)}, f32[2,560,128]{2,1,0:T(8,128)S(1)}, u32[]{:S(2)}, u32[]{:S(2)}) collective-permute-start(f32[2,560,128]{2,1,0:T(8,128)S(1)} %pad_maximum_fusion), channel_id=1, source_target_pairs={{0,8},{8,16},{16,24},{1,9},{9,17},{17,25},{2,10},{10,18},{18,26},{... | collective-permute-start | bytes 1720328 | tf_op jit(solution)/shard_map/ppermute | solution.py:337
  103.5 11.0 %collective-permute-start.11 = (f32[2,560,128]{2,1,0:T(8,128)S(1)}, f32[2,560,128]{2,1,0:T(8,128)S(1)}, u32[]{:S(2)}, u32[]{:S(2)}) collective-permute-start(f32[2,560,128]{2,1,0:T(8,128)S(1)} %pad_maximum_fusion.1), channel_id=1, source_target_pairs={{8,0},{16,8},{24,16},{9,1},{17,9},{25,17},{10,2},{18,10},{26,18},{... | collective-permute-start | bytes 1720328 | tf_op jit(solution)/shard_map/ppermute | solution.py:337
  110.1 4.5 %copy-start = (f32[2,560,128]{2,1,0:T(8,128)}, f32[2,560,128]{2,1,0:T(8,128)S(1)}, u32[]{:S(2)}) copy-start(f32[2,560,128]{2,1,0:T(8,128)S(1)} %collective-permute-done.10.up_ref) | copy-start | bytes 1720324
  114.5 0.8 copy-start.1

commit v2 on v1

--- a/solution.py
+++ b/solution.py
@@ -39,27 +39,21 @@
 
 
 def taper_weights(squared):
-    inverse = lax.rsqrt(jnp.maximum(squared, 1.0))
-    ratio = squared * inverse * (1.0 / HALFW)
-    outer_inverse = (2.0 * HALFW / 3.0) * inverse
-    inner = (((-0.25 * ratio + 0.5) * ratio + 0.625) * ratio - 5.0 / 3.0) * ratio * ratio + 1.0
-    outer = (
-        ((((ratio * (1.0 / 12.0) - 0.5) * ratio + 0.625) * ratio + 5.0 / 3.0) * ratio - 5.0) * ratio
-        + 4.0
-        - outer_inverse
-    )
-    return jnp.where(ratio <= 1.0, inner, jnp.where(ratio < 2.0, outer, 0.0))
-
-
-def place(cols_count):
-    return lax.axis_index("rows"), lax.axis_index("cols")
-
-
-def gather_kernel(width, order, cells, weight_ref, prior_ref, out_ref, picked):
+    inverse = lax.rsqrt(jnp.maximum(squared, 1e-4))
+    ratio = squared * inverse
+    inner = 1.0 - (ratio * ratio) * (5.0 / 3.0 - ratio * (0.625 + ratio * (0.5 - 0.25 * ratio)))
+    left = jnp.maximum(2.0 - ratio, 0.0)
+    left = left * left
+    outer = (left * left) * (((ratio + 2.0) * ratio - 0.5) * (inverse * (1.0 / 12.0)))
+    return jnp.where(ratio <= 1.0, inner, outer)
+
+
+def gather_kernel(width, order, cells, weight_ref, prior_ref, kept_ref, sent_ref, picked):
     height, cols = prior_ref.shape[0], prior_ref.shape[1]
     my_row, my_col = lax.axis_index("rows"), lax.axis_index("cols")
     mine = 2 * lax.rem(my_row, 2) + lax.rem(lax.div(my_row, 2), 2)
-    out_ref[...] = jnp.zeros_like(out_ref)
+    kept_ref[...] = jnp.zeros_like(kept_ref)
+    sent_ref[...] = jnp.zeros_like(sent_ref)
     for k in range(BATCHES):
         batch = order[k]
         first = cells[batch, 0]
@@ -77,7 +71,7 @@
                 return carry
 
             lax.fori_loop(0, OBS, one, 0, unroll=8)
-            weights = weight_ref[batch]
+            weights = jnp.transpose(weight_ref[batch])
             low = low_lanes((OBS, 2 * MEMBERS))
             total = jnp.zeros((OBS, 2 * MEMBERS), F32)
             for p in range(SPECIES // 2):
@@ -86,17 +80,24 @@
             total = total + swap_halves(total)
             slot = jnp.bitwise_xor(k % 4, mine)
             keep = low if k < 4 else jnp.logical_not(low)
-            out_ref[slot] = jnp.where(keep, total, out_ref[slot])
-
-
-def exchange(parts):
+
+            @pl.when(slot < 2)
+            def _():
+                kept_ref[slot] = jnp.where(keep, total, kept_ref[slot])
+
+            @pl.when(slot >= 2)
+            def _():
+                sent_ref[slot - 2] = jnp.where(keep, total, sent_ref[slot - 2])
+
+
+def exchange(kept, sent):
     size = lax.axis_size("rows")
     cols = lax.axis_size("cols")
 
     def rows(x, bit):
         return lax.ppermute(x, "rows", [(i, i ^ bit) for i in range(size)])
 
-    kept = parts[:2] + rows(parts[2:], 1)
+    kept = kept + rows(sent, 1)
     kept = kept[0] + rows(kept[1], 2)
     bit = 4
     while bit < size:
@@ -112,7 +113,7 @@
 
 def main_kernel(
     width, order, cells, mask, cell_ref, value_ref, var_ref, prior_ref, p0, p1, p2, p3,
-    out_ref, left_ref, right_ref, predicted, table,
+    out_ref, first_ref, second_ref, predicted, table,
 ):
     height, cols = prior_ref.shape[0], prior_ref.shape[1]
     my_row, my_col = lax.axis_index("rows"), lax.axis_index("cols")
@@ -138,18 +139,20 @@
         table[16 + k : 17 + k, :] = var_ref[pl.ds(batches[k], 1), :]
     cell_lane = table[0:8, :]
     row_lane = jnp.floor(cell_lane * (1.0 / width))
-    col_lane = cell_lane - row_lane * width
+    col_lane = (cell_lane - row_lane * width) * (1.0 / HALFW)
+    row_lane = row_lane * (1.0 / HALFW)
     row_col = jnp.transpose(row_lane)
     col_col = jnp.transpose(col_lane)
     value_col = jnp.transpose(table[8:16, :])
     var_col = jnp.transpose(table[16:24, :])
     low_obs = low_lanes((OBS, 2 * MEMBERS))
-    x_pos = (my_col * cols + lax.broadcasted_iota(jnp.int32, (cols, OBS), 0)).astype(F32)
-
-    def update(x, taper, spread_w, spread_lo, gain_w, gain_hi):
+    x_pos = (my_col * cols + lax.broadcasted_iota(jnp.int32, (cols, OBS), 0)).astype(F32) * (
+        1.0 / HALFW
+    )
+
+    def update(x, taper, spread_w, gain_w, gain_hi):
         high, low_part = split(x)
-        cov = dot(jnp.concatenate([high, low_part], 1), spread_w) + dot(high, spread_lo)
-        c_high, c_low = split(cov * taper)
+        c_high, c_low = split(dot(jnp.concatenate([high, low_part, high], 1), spread_w) * taper)
         both = dot(c_high, gain_w)
         return x + (both[:, : 2 * MEMBERS] + both[:, 2 * MEMBERS :] + dot(c_low, gain_hi))
 
@@ -173,7 +176,7 @@
         zero = jnp.zeros_like(turned)
         wide = jnp.concatenate([jnp.where(top, turned, zero), jnp.where(top, zero, turned)], 1)
         wide_hi, wide_lo = split(wide)
-        spread_w = jnp.concatenate([wide_hi, wide_hi], 0)
+        spread_w = jnp.concatenate([wide_hi, wide_hi, wide_lo], 0)
         tall = jnp.concatenate([jnp.where(low_obs, gain, zero), jnp.where(low_obs, zero, gain)], 0)
         tall_hi, tall_lo = split(tall)
         gain_w = jnp.concatenate([tall_hi, tall_lo], 1)
@@ -189,82 +192,82 @@
                     active = (mask[batches[k], tiles[later]] > 0).astype(F32)
                     halves.append(taper_weights(dr * dr + dc * dc) * active)
                 predicted[q] = update(
-                    predicted[q], jnp.concatenate(halves, 1), spread_w, wide_lo, gain_w, tall_hi
+                    predicted[q], jnp.concatenate(halves, 1), spread_w, gain_w, tall_hi
                 )
 
-        @pl.when(mask[batches[k], my_tile] > 0)
-        def _():
-            dx = x_pos - obs_col
-            dx = dx * dx
-
-            def pair(j, carry):
-                halves = []
-                for h in range(2):
-                    dy = (my_row * height + 2 * j + h).astype(F32) - obs_row
-                    halves.append(taper_weights(dx + dy * dy))
-                taper = jnp.concatenate(halves, 1)
-                taper = jnp.concatenate([taper] * SPECIES, 0)
-                out_ref[j] = update(out_ref[j], taper, spread_w, wide_lo, gain_w, tall_hi)
-                return carry
-
-            lax.fori_loop(0, height // 2, pair, 0)
-
+        active = (mask[batches[k], my_tile] > 0).astype(F32)
+        dx = x_pos - obs_col
+        dx = dx * dx
+        for j in range(height // 2):
+            halves = []
+            for h in range(2):
+                dy = (my_row * height + 2 * j + h).astype(F32) * (1.0 / HALFW) - obs_row
+                halves.append(taper_weights(dx + dy * dy) * active)
+            taper = jnp.concatenate([jnp.concatenate(halves, 1)] * SPECIES, 0)
+            out_ref[j] = update(out_ref[j], taper, spread_w, gain_w, tall_hi)
+
+    even = lax.rem(my_col, 2) == 0
     for j in range(height // 2):
         for e in range(HALO):
             for t in range(SPECIES):
-                left_ref[j, e, t : t + 1, :] = out_ref[j, t * cols + e : t * cols + e + 1, :]
+                r = t * cols + e
+                a = out_ref[j, r : r + 1, :]
                 r = t * cols + cols - HALO + e
-                right_ref[j, e, t : t + 1, :] = out_ref[j, r : r + 1, :]
-
-
-def smooth_kernel(kern, mix, tile_ref, left_ref, right_ref, up_ref, down_ref, out_ref, padded, lines):
+                b = out_ref[j, r : r + 1, :]
+                first_ref[j, e, t : t + 1, :] = jnp.where(even, b, a)
+                second_ref[j, e, t : t + 1, :] = jnp.where(even, a, b)
+
+
+def smooth_kernel(
+    kern, mix, tile_ref, side0_ref, side1_ref, rows0_ref, rows1_ref, out_ref, padded, lines
+):
     pairs, cols = tile_ref.shape[0], tile_ref.shape[1] // SPECIES
     depth = cols + 16
     lanes = 2 * MEMBERS
-    half = 3 * SPECIES
+    even_row = lax.rem(lax.axis_index("rows"), 2) == 0
+    even_col = lax.rem(lax.axis_index("cols"), 2) == 0
     edge = jnp.zeros((8, lanes), F32)
+
     for q in range(pairs + 4):
+        inside = 2 <= q < pairs + 2
+        p = q - 2 if inside else (q if q < 2 else q - pairs - 2)
+
+        def outside(lo, hi):
+            a, b = rows0_ref[p, lo:hi, :], rows1_ref[p, lo:hi, :]
+            return jnp.where(even_row, b, a) if q < 2 else jnp.where(even_row, a, b)
+
         for t in range(SPECIES):
             padded[q, t, 0:8, :] = edge
             padded[q, t, depth - 8 : depth, :] = edge
-            if q < 2:
-                body = up_ref[q, t * cols : (t + 1) * cols, :]
-            elif q < pairs + 2:
-                body = tile_ref[q - 2, t * cols : (t + 1) * cols, :]
-            else:
-                body = down_ref[q - pairs - 2, t * cols : (t + 1) * cols, :]
-            padded[q, t, 8 : 8 + cols, :] = body
+            lo, hi = t * cols, (t + 1) * cols
+            padded[q, t, 8 : 8 + cols, :] = tile_ref[p, lo:hi, :] if inside else outside(lo, hi)
             for e in range(HALO):
-                at = e * SPECIES + t
-                base = SPECIES * cols
-                if q < 2:
-                    a = up_ref[q, base + at : base + at + 1, :]
-                    b = up_ref[q, base + half + at : base + half + at + 1, :]
-                elif q < pairs + 2:
-                    a = left_ref[q - 2, e, t : t + 1, :]
-                    b = right_ref[q - 2, e, t : t + 1, :]
+                if inside:
+                    a, b = side0_ref[p, e, t : t + 1, :], side1_ref[p, e, t : t + 1, :]
                 else:
-                    a = down_ref[q - pairs - 2, base + at : base + at + 1, :]
-                    b = down_ref[q - pairs - 2, base + half + at : base + half + at + 1, :]
-                padded[q, t, 5 + e : 6 + e, :] = a
-                padded[q, t, 8 + cols + e : 9 + cols + e, :] = b
-    offset = lax.broadcasted_iota(jnp.int32, (cols, depth), 1) - (
-        lax.broadcasted_iota(jnp.int32, (cols, depth), 0) + 5
-    )
+                    at = SPECIES * cols + e * SPECIES + t
+                    a = outside(at, at + 1)
+                    b = outside(at + HALO * SPECIES, at + HALO * SPECIES + 1)
+                padded[q, t, 5 + e : 6 + e, :] = jnp.where(even_col, b, a)
+                padded[q, t, 8 + cols + e : 9 + cols + e, :] = jnp.where(even_col, a, b)
+    column = lax.broadcasted_iota(jnp.int32, (cols, 3 * depth), 1)
+    third = column >= 2 * depth
+    column = jnp.where(third, column - 2 * depth, jnp.where(column >= depth, column - depth, column))
+    offset = column - (lax.broadcasted_iota(jnp.int32, (cols, 3 * depth), 0) + 5)
     low = low_lanes((cols, lanes))
 
     def species(t, carry):
         bands = []
         for a in range(KW):
-            band = jnp.zeros((cols, depth), F32)
+            band = jnp.zeros((cols, 3 * depth), F32)
             for e in range(KW):
                 band = jnp.where(offset == e, kern[t, a * KW + e], band)
-            bands.append(band)
-        band_hi, band_lo = split(jnp.concatenate(bands, 0))
+            high = band.astype(BF16).astype(F32)
+            bands.append(jnp.where(third, band - high, high).astype(BF16))
+        band = jnp.concatenate(bands, 0)
         for d in range(0, pairs + 4, 2):
-            data = jnp.concatenate([padded[d, t], padded[d + 1, t]], 1)
-            hi, lo = split(data)
-            product = dot(band_hi, hi) + dot(band_hi, lo) + dot(band_lo, hi)
+            hi, lo = split(jnp.concatenate([padded[d, t], padded[d + 1, t]], 1))
+            product = dot(band, jnp.concatenate([hi, lo, hi], 0))
             lines[d] = product[:, :lanes]
             lines[d + 1] = product[:, lanes:]
 
@@ -308,17 +311,17 @@
     width = cols * across
     pairs = height // 2
     lanes = 2 * MEMBERS
-    parts = pl.pallas_call(
+    kept, sent = pl.pallas_call(
         functools.partial(gather_kernel, width),
-        out_shape=jax.ShapeDtypeStruct((4, OBS, lanes), F32),
+        out_shape=(jax.ShapeDtypeStruct((2, OBS, lanes), F32),) * 2,
         in_specs=[SMEM, SMEM, VMEM, VMEM],
-        out_specs=VMEM,
+        out_specs=(VMEM, VMEM),
         scratch_shapes=[pltpu.VMEM((OBS, channels), F32)],
         compiler_params=PARAMS,
         name="gather",
-    )(batch_order, obs_cell, obs_weight, prior)
-    arrived = exchange(parts)
-    tile, left, right = pl.pallas_call(
+    )(batch_order, obs_cell, jnp.transpose(obs_weight, (0, 2, 1)), prior)
+    arrived = exchange(kept, sent)
+    tile, first, second = pl.pallas_call(
         functools.partial(main_kernel, width),
         out_shape=(
             jax.ShapeDtypeStruct((pairs, SPECIES * cols, lanes), F32),
@@ -332,23 +335,23 @@
         name="assimilate",
     )(batch_order, obs_cell, loc_mask, obs_cell, obs_value, obs_var, prior, *arrived)
 
-    def shift(x, axis, step):
+    def swap(x, axis, start):
         size = lax.axis_size(axis)
-        return lax.ppermute(
-            x, axis, [(i, i + step) for i in range(size) if 0 <= i + step < size]
-        )
-
-    from_left = shift(right, "cols", 1)
-    from_right = shift(left, "cols", -1)
+        pairs_of = [(i, i + 1) for i in range(start, size - 1, 2)]
+        return lax.ppermute(x, axis, pairs_of + [(j, i) for i, j in pairs_of])
+
+    side0, side1 = swap(first, "cols", 0), swap(second, "cols", 1)
 
     def with_sides(lo, hi):
         flat = (hi - lo, HALO * SPECIES, lanes)
         return jnp.concatenate(
-            [tile[lo:hi], from_left[lo:hi].reshape(flat), from_right[lo:hi].reshape(flat)], 1
+            [tile[lo:hi], side0[lo:hi].reshape(flat), side1[lo:hi].reshape(flat)], 1
         )
 
-    above = shift(with_sides(pairs - 2, pairs), "rows", 1)
-    below = shift(with_sides(0, 2), "rows", -1)
+    even = lax.rem(lax.axis_index("rows"), 2) == 0
+    bottom, top = with_sides(pairs - 2, pairs), with_sides(0, 2)
+    rows0 = swap(jnp.where(even, bottom, top), "rows", 0)
+    rows1 = swap(jnp.where(even, top, bottom), "rows", 1)
     return pl.pallas_call(
         smooth_kernel,
         out_shape=jax.ShapeDtypeStruct((height, cols, channels), F32),
@@ -360,7 +363,7 @@
         ],
         compiler_params=PARAMS,
         name="smooth",
-    )(kernel.reshape(SPECIES, KW * KW), mixing, tile, from_left, from_right, above, below)
+    )(kernel.reshape(SPECIES, KW * KW), mixing, tile, side0, side1, rows0, rows1)
 
 
 def solution(mesh):

time: 132 us -> 90.8 us (0.69)
  the two profiles are of different devices: /device:TPU:11 before, /device:TPU:9 now
where the time goes in v2:
time: 90.8 us; the launch traced here: 89.5 us
  Pallas kernels  39.8 us (44%)
  waiting for transfers between devices  22.7 us (25%)
  starting transfers between devices  21.6 us (24%)
  local copies, waits for them, and re-layouts  4.22 us (5%)
  other arithmetic  1.04 us (1%)
    pallas_call x1, Pallas kernels, shards(): pl.pallas_call(functools.partial(main_kernel, width), out_shape=(jax.Shap...  24.3 us
    pallas_call x1, Pallas kernels, shards(): pl.pallas_call(smooth_kernel, out_shape=jax.ShapeDtypeStruct((height, col...  11.5 us
    ppermute x5, starting transfers between devices, rows(): return lax.ppermute(x, 'rows', [(i, i ^ bit) for i in range(size)])  10.3 us
    ppermute x4, waiting for transfers between devices, swap(): return lax.ppermute(x, axis, pairs_of + [(j, i) for i, j in pairs_of])  9.84 us
    ppermute x4, starting transfers between devices, swap(): return lax.ppermute(x, axis, pairs_of + [(j, i) for i, j in pairs_of])  9.05 us
    ppermute x3, waiting for transfers between devices, exchange(): lax.ppermute(kept, 'cols', [(i, i ^ bit) for i in range(cols)])  8.2 us
    ppermute x5, waiting for transfers between devices, rows(): return lax.ppermute(x, 'rows', [(i, i ^ bit) for i in range(size)])  4.63 us
    pallas_call x1, Pallas kernels, shards(): pl.pallas_call(functools.partial(gather_kernel, width), out_shape=(jax.Sh...  4.13 us
  transfers between devices with their start and end apart: 12, of which 8 were waited for; matrix products, arithmetic and copies ran while one was open for 2% of the time, Pallas kernels for 0%

profile of v2, /device:TPU:9, one launch (start us, length us, event | category | flops | bytes accessed | tf_op | source)
XLA Modules:
  0.0 89.5 jit_solution(4610132265966956934)
XLA Ops:
  0.0 4.1 %gather.1 = (f32[2,128,128]{2,1,0:T(8,128)}, f32[2,128,128]{2,1,0:T(8,128)}) custom-call(s32[8]{0:T(128)} %order.3, s32[8,128]{1,0:T(8,128)} %cell_ref.1, f32[8,8,128]{2,1,0:T(8,128)} %bitcast.15, f32[16,64,512]{2,1,0:T(8,128)} %prior_ref.3), custom_call_target="tpu_custom_call" | custom-call | tf_op jit(solution)/shard_map/gather/pallas_call | solution.py:314
  4.1 0.0 collective-permute-start
  4.1 1.6 %collective-permute-done = f32[2,128,128]{2,1,0:T(8,128)S(1)} collective-permute-done((f32[2,128,128]{2,1,0:T(8,128)}, f32[2,128,128]{2,1,0:T(8,128)S(1)}, u32[]{:S(2)}, u32[]{:S(2)}) %collective-permute-start) | collective-permute-done | bytes 131104 | tf_op jit(solution)/shard_map/ppermute | solution.py:98
  5.7 0.9 %add.15 = f32[2,128,128]{2,1,0:T(8,128)S(1)} add(f32[2,128,128]{2,1,0:T(8,128)} %get-tuple-element.10, f32[2,128,128]{2,1,0:T(8,128)S(1)} %collective-permute-done) | non-fusion elementwise | flops 32768 | bytes 393216 | tf_op jit(solution)/shard_map/add | solution.py:100
  6.6 1.6 %collective-permute-start.1 = (f32[128,128]{1,0:T(8,128)S(1)}, f32[128,128]{1,0:T(8,128)S(1)}, u32[]{:S(2)}, u32[]{:S(2)}) collective-permute-start(f32[128,128]{1,0:T(8,128)S(1)} %slice_bitcast_fusion), channel_id=1, source_target_pairs={{0,16},{8,24},{16,0},{24,8},{1,17},{9,25},{17,1},{25,9},{2,18},{10... | collective-permute-start | bytes 196616 | tf_op jit(solution)/shard_map/ppermute | solution.py:98
  8.3 2.2 %collective-permute-done.1 = f32[128,128]{1,0:T(8,128)S(1)} collective-permute-done((f32[128,128]{1,0:T(8,128)S(1)}, f32[128,128]{1,0:T(8,128)S(1)}, u32[]{:S(2)}, u32[]{:S(2)}) %collective-permute-start.1) | collective-permute-done | bytes 65568 | tf_op jit(solution)/shard_map/ppermute | solution.py:98
  10.4 1.3 %collective-permute-start.2 = (f32[128,128]{1,0:T(8,128)S(1)}, f32[128,128]{1,0:T(8,128)S(1)}, u32[]{:S(2)}, u32[]{:S(2)}) collective-permute-start(f32[128,128]{1,0:T(8,128)S(1)} %fusion.2), channel_id=1, source_target_pairs={{0,1},{1,0},{2,3},{3,2},{4,5},{5,4},{6,7},{7,6},{8,9},{9,8},{10,11... | collective-permute-start | bytes 196616 | tf_op jit(solution)/shard_map/ppermute | solution.py:108
  11.7 1.9 %collective-permute-done.2 = f32[128,128]{1,0:T(8,128)S(1)} collective-permute-done((f32[128,128]{1,0:T(8,128)S(1)}, f32[128,128]{1,0:T(8,128)S(1)}, u32[]{:S(2)}, u32[]{:S(2)}) %collective-permute-start.2) | collective-permute-done | bytes 65568 | tf_op jit(solution)/shard_map/ppermute | solution.py:108
  13.6 0.1 collective-permute-start.3
  13.7 3.1 %collective-permute-done.3 = f32[128,128]{1,0:T(8,128)S(1)} collective-permute-done((f32[128,128]{1,0:T(8,128)S(1)}, f32[128,128]{1,0:T(8,128)S(1)}, u32[]{:S(2)}, u32[]{:S(2)}) %collective-permute-start.3) | collective-permute-done | bytes 65568 | tf_op jit(solution)/shard_map/ppermute | solution.py:108
  16.8 0.9 %collective-permute-start.4 = (f32[128,128]{1,0:T(8,128)S(1)}, f32[128,128]{1,0:T(8,128)S(1)}, u32[]{:S(2)}, u32[]{:S(2)}) collective-permute-start(f32[128,128]{1,0:T(8,128)S(1)} %add.18), channel_id=1, source_target_pairs={{0,4},{1,5},{2,6},{3,7},{4,0},{5,1},{6,2},{7,3},{8,12},{9,13},{10,... | collective-permute-start | bytes 196616 | tf_op jit(solution)/shard_map/ppermute | solution.py:108
  17.7 3.2 %collective-permute-done.4 = f32[128,128]{1,0:T(8,128)S(1)} collective-permute-done((f32[128,128]{1,0:T(8,128)S(1)}, f32[128,128]{1,0:T(8,128)S(1)}, u32[]{:S(2)}, u32[]{:S(2)}) %collective-permute-start.4) | collective-permute-done | bytes 65568 | tf_op jit(solution)/shard_map/ppermute | solution.py:108
  20.9 1.3 %collective-permute-start.5 = (f32[128,128]{1,0:T(8,128)S(1)}, f32[128,128]{1,0:T(8,128)S(1)}, u32[]{:S(2)}, u32[]{:S(2)}) collective-permute-start(f32[128,128]{1,0:T(8,128)S(1)} %add.19.p0), channel_id=1, source_target_pairs={{0,16},{8,24},{16,0},{24,8},{1,17},{9,25},{17,1},{25,9},{2,18},{10... | collective-permute-start | bytes 196616 | tf_op jit(solution)/shard_map/ppermute | solution.py:98
  22.2 4.9 %collective-permute-start.6 = (f32[128,128]{1,0:T(8,128)S(1)}, f32[128,128]{1,0:T(8,128)S(1)}, u32[]{:S(2)}, u32[]{:S(2)}) collective-permute-start(f32[128,128]{1,0:T(8,128)S(1)} %add.19.p0), channel_id=1, source_target_pairs={{0,8},{8,0},{16,24},{24,16},{1,9},{9,1},{17,25},{25,17},{2,10},{10... | collective-permute-start | bytes 196616 | tf_op jit(solution)/shard_map/ppermute | solution.py:98
  27.2 2.4 %collective-permute-start.7 = (f32[128,128]{1,0:T(8,128)S(1)}, f32[128,128]{1,0:T(8,128)S(1)}, u32[]{:S(2)}, u32[]{:S(2)}) collective-permute-start(f32[128,128]{1,0:T(8,128)S(1)} %collective-permute-done.5.p1), channel_id=1, source_target_pairs={{0,8},{8,0},{16,24},{24,16},{1,9},{9,1},{17,25},{25,17},{2,10},{10... | collective-permute-start | bytes 196616 | tf_op jit(solution)/shard_map/ppermute | solution.py:98
  29.6 0.9 %collective-permute-done.7.p3 = f32[128,128]{1,0:T(8,128)S(1)} collective-permute-done((f32[128,128]{1,0:T(8,128)S(1)}, f32[128,128]{1,0:T(8,128)S(1)}, u32[]{:S(2)}, u32[]{:S(2)}) %collective-permute-start.7) | collective-permute-done | bytes 65568 | tf_op jit(solution)/shard_map/ppermute | solution.py:98
  30.5 0.6 copy-done.7
  31.1 24.3 %assimilate.1 = (f32[8,512,128]{2,1,0:T(8,128)}, f32[8,3,8,128]{3,2,1,0:T(8,128)}, f32[8,3,8,128]{3,2,1,0:T(8,128)}) custom-call(s32[8]{0:T(128)} %order.3, s32[8,128]{1,0:T(8,128)} %cell_ref.1, s32[8,32]{1,0:T(8,128)} %mask.1, s32[8,128]{1,0:T(8,128)} %cell_ref.1, f32[8,128]{1,0:T(8,128)} %value_ref.1, f32[8,128]{1,0:T(8,128)} %var_ref.1, ...), custom_call_target="tpu_custom_call" | custom-call | tf_op jit(solution)/shard_map/assimilate/pallas_call | solution.py:324
  55.4 1.7 %collective-permute-start.8 = (f32[8,3,8,128]{3,2,1,0:T(8,128)}, f32[8,3,8,128]{3,2,1,0:T(8,128)S(1)}, u32[]{:S(2)}, u32[]{:S(2)}) collective-permute-start(f32[8,3,8,128]{3,2,1,0:T(8,128)} %get-tuple-element.13), channel_id=1, source_target_pairs={{0,1},{2,3},{4,5},{6,7},{1,0},{3,2},{5,4},{7,6},{8,9},{10,11},{12,... | collective-permute-start | bytes 294920 | tf_op jit(solution)/shard_map/ppermute | solution.py:341
  57.1 1.9 %collective-permute-start.9 = (f32[8,3,8,128]{3,2,1,0:T(8,128)}, f32[8,3,8,128]{3,2,1,0:T(8,128)S(1)}, u32[]{:S(2)}, u32[]{:S(2)}) collective-permute-start(f32[8,3,8,128]{3,2,1,0:T(8,128)} %get-tuple-element.14), channel_id=1, source_target_pairs={{1,2},{3,4},{5,6},{2,1},{4,3},{6,5},{9,10},{11,12},{13,14},{10,9},... | collective-permute-start | bytes 294920 | tf_op jit(solution)/shard_map/ppermute | solution.py:341
  59.0 0.0 copy-start.8
  59.1 1.3 %fusion.3 = (f32[2,512,128]{2,1,0:T(8,128)S(1)}, f32[2,512,128]{2,1,0:T(8,128)S(1)}) fusion(f32[8,512,128]{2,1,0:T(8,128)} %get-tuple-element.12.tile_ref), kind=kLoop, calls=%fused_computation.11 | loop fusion | bytes 2097152 | tf_op jit(solution)/shard_map/slice | solution.py:348
  60.3 0.0 collective-permute-done.8.side0_ref
  60.4 3.2 %collective-permute-done.9.side1_ref = f32[8,3,8,128]{3,2,1,0:T(8,128)S(1)} collective-permute-done((f32[8,3,8,128]{3,2,1,0:T(8,128)}, f32[8,3,8,128]{3,2,1,0:T(8,128)S(1)}, u32[]{:S(2)}, u32[]{:S(2)}) %collective-permute-start.9) | collective-permute-done | bytes 98336 | tf_op jit(solution)/shard_map/ppermute | solution.py:341
  63.6 0.1 fusion
  63.7 5.3 %collective-permute-start.11 = (f32[2,560,128]{2,1,0:T(8,128)S(1)}, f32[2,560,128]{2,1,0:T(8,128)S(1)}, u32[]{:S(2)}, u32[]{:S(2)}) collective-permute-start(f32[2,560,128]{2,1,0:T(8,128)S(1)} %get-tuple-element.17), channel_id=1, source_target_pairs={{8,16},{16,8},{9,17},{17,9},{10,18},{18,10},{11,19},{19,11},{12,20... | collective-permute-start | bytes 1720328 | tf_op jit(solution)/shard_map/ppermute | solution.py:341
  69.0 0.1 collective-permute-start.10
  69.1 0.7 reshape.15.kern
  69.8 6.6 %collective-permute-done.11.rows1_ref = f32[2,560,128]{2,1,0:T(8,128)S(1)} collective-permute-done((f32[2,560,128]{2,1,0:T(8,128)S(1)}, f32[2,560,128]{2,1,0:T(8,128)S(1)}, u32[]{:S(2)}, u32[]{:S(2)}) %collective-permute-start.11) | collective-permute-done | bytes 573472 | tf_op jit(solution)/shard_map/ppermute | solution.py:341
  76.4 0.8 copy-done
  77.2 0.8 copy-done.1
  78.0 11.5 %smooth.1 = f32[16,64,512]{2,1,0:T(8,128)} custom-call(f32[8,49]{1,0:T(8,128)} %reshape.15.kern, f32[8,8]{1,0:T(8,128)} %mix.1, f32[8,512,128]{2,1,0:T(8,128)} %get-tuple-element.12.tile_ref, f32[8,3,8,128]{3,2,1,0:T(8,128)} %copy-done.3, f32[8,3,8,128]{3,2,1,0:T(8,128)} %copy-done.4, f32[2,560,128]{2,1,0:T(8,128)} %copy-done.1, f32[2,560,128]{2,1,0:T(8,128)} %copy-done), custom_call_target="tpu_custom_call" | custom-call | tf_op jit(solution)/shard_map/smooth/pallas_call | solution.py:355
  (25 shorter events, 0.1 us)
Async XLA Ops:
  4.1 1.6 %collective-permute-start = (f32[2,128,128]{2,1,0:T(8,128)}, f32[2,128,128]{2,1,0:T(8,128)S(1)}, u32[]{:S(2)}, u32[]{:S(2)}) collective-permute-start(f32[2,128,128]{2,1,0:T(8,128)} %get-tuple-element.11), channel_id=1, source_target_pairs={{0,8},{8,0},{16,24},{24,16},{1,9},{9,1},{17,25},{25,17},{2,10},{10... | collective-permute-start | bytes 393224 | tf_op jit(solution)/shard_map/ppermute | solution.py:98
  6.6 3.8 %collective-permute-start.1 = (f32[128,128]{1,0:T(8,128)S(1)}, f32[128,128]{1,0:T(8,128)S(1)}, u32[]{:S(2)}, u32[]{:S(2)}) collective-permute-start(f32[128,128]{1,0:T(8,128)S(1)} %slice_bitcast_fusion), channel_id=1, source_target_pairs={{0,16},{8,24},{16,0},{24,8},{1,17},{9,25},{17,1},{25,9},{2,18},{10... | collective-permute-start | bytes 196616 | tf_op jit(solution)/shard_map/ppermute | solution.py:98
  10.4 3.2 %collective-permute-start.2 = (f32[128,128]{1,0:T(8,128)S(1)}, f32[128,128]{1,0:T(8,128)S(1)}, u32[]{:S(2)}, u32[]{:S(2)}) collective-permute-start(f32[128,128]{1,0:T(8,128)S(1)} %fusion.2), channel_id=1, source_target_pairs={{0,1},{1,0},{2,3},{3,2},{4,5},{5,4},{6,7},{7,6},{8,9},{9,8},{10,11... | collective-permute-start | bytes 196616 | tf_op jit(solution)/shard_map/ppermute | solution.py:108
  13.6 3.2 %collective-permute-start.3 = (f32[128,128]{1,0:T(8,128)S(1)}, f32[128,128]{1,0:T(8,128)S(1)}, u32[]{:S(2)}, u32[]{:S(2)}) collective-permute-start(f32[128,128]{1,0:T(8,128)S(1)} %add.17), channel_id=1, source_target_pairs={{0,2},{1,3},{2,0},{3,1},{4,6},{5,7},{6,4},{7,5},{8,10},{9,11},{10,... | collective-permute-start | bytes 196616 | tf_op jit(solution)/shard_map/ppermute | solution.py:108
  16.8 4.1 %collective-permute-start.4 = (f32[128,128]{1,0:T(8,128)S(1)}, f32[128,128]{1,0:T(8,128)S(1)}, u32[]{:S(2)}, u32[]{:S(2)}) collective-permute-start(f32[128,128]{1,0:T(8,128)S(1)} %add.18), channel_id=1, source_target_pairs={{0,4},{1,5},{2,6},{3,7},{4,0},{5,1},{6,2},{7,3},{8,12},{9,13},{10,... | collective-permute-start | bytes 196616 | tf_op jit(solution)/shard_map/ppermute | solution.py:108
  20.9 9.6 %copy-start.2 = (f32[128,128]{1,0:T(8,128)}, f32[128,128]{1,0:T(8,128)S(1)}, u32[]{:S(2)}) copy-start(f32[128,128]{1,0:T(8,128)S(1)} %add.19.p0) | copy-start | bytes 196612
  20.9 6.2 %collective-permute-start.5 = (f32[128,128]{1,0:T(8,128)S(1)}, f32[128,128]{1,0:T(8,128)S(1)}, u32[]{:S(2)}, u32[]{:S(2)}) collective-permute-start(f32[128,128]{1,0:T(8,128)S(1)} %add.19.p0), channel_id=1, source_target_pairs={{0,16},{8,24},{16,0},{24,8},{1,17},{9,25},{17,1},{25,9},{2,18},{10... | collective-permute-start | bytes 196616 | tf_op jit(solution)/shard_map/ppermute | solution.py:98
  22.2 7.3 %collective-permute-start.6 = (f32[128,128]{1,0:T(8,128)S(1)}, f32[128,128]{1,0:T(8,128)S(1)}, u32[]{:S(2)}, u32[]{:S(2)}) collective-permute-start(f32[128,128]{1,0:T(8,128)S(1)} %add.19.p0), channel_id=1, source_target_pairs={{0,8},{8,0},{16,24},{24,16},{1,9},{9,1},{17,25},{25,17},{2,10},{10... | collective-permute-start | bytes 196616 | tf_op jit(solution)/shard_map/ppermute | solution.py:98
  27.2 3.3 %copy-start.5 = (f32[128,128]{1,0:T(8,128)}, f32[128,128]{1,0:T(8,128)S(1)}, u32[]{:S(2)}) copy-start(f32[128,128]{1,0:T(8,128)S(1)} %collective-permute-done.5.p1) | copy-start | bytes 196612
  27.2 3.3 %collective-permute-start.7 = (f32[128,128]{1,0:T(8,128)S(1)}, f32[128,128]{1,0:T(8,128)S(1)}, u32[]{:S(2)}, u32[]{:S(2)}) collective-permute-start(f32[128,128]{1,0:T(8,128)S(1)} %collective-permute-done.5.p1), channel_id=1, source_target_pairs={{0,8},{8,0},{16,24},{24,16},{1,9},{9,1},{17,25},{25,17},{2,10},{10... | collective-permute-start | bytes 196616 | tf_op jit(solution)/shard_map/ppermute | solution.py:98
  29.6 0.9 %copy-start.6 = (f32[128,128]{1,0:T(8,128)}, f32[128,128]{1,0:T(8,128)S(1)}, u32[]{:S(2)}) copy-start(f32[128,128]{1,0:T(8,128)S(1)} %collective-permute-done.6.p2) | copy-start | bytes 196612
  30.5 0.6 copy-start.7
  55.4 5.0 %collective-permute-start.8 = (f32[8,3,8,128]{3,2,1,0:T(8,128)}, f32[8,3,8,128]{3,2,1,0:T(8,128)S(1)}, u32[]{:S(2)}, u32[]{:S(2)}) collective-permute-start(f32[8,3,8,128]{3,2,1,0:T(8,128)} %get-tuple-element.13), channel_id=1, source_target_pairs={{0,1},{2,3},{4,5},{6,7},{1,0},{3,2},{5,4},{7,6},{8,9},{10,11},{12,... | collective-permute-start | bytes 294920 | tf_op jit(solution)/shard_map/ppermute | solution.py:341
  57.1 6.5 %collective-permute-start.9 = (f32[8,3,8,128]{3,2,1,0:T(8,128)}, f32[8,3,8,128]{3,2,1,0:T(8,128)S(1)}, u32[]{:S(2)}, u32[]{:S(2)}) collective-permute-start(f32[8,3,8,128]{3,2,1,0:T(8,128)} %get-tuple-element.14), channel_id=1, source_target_pairs={{1,2},{3,4},{5,6},{2,1},{4,3},{6,5},{9,10},{11,12},{13,14},{10,9},... | collective-permute-start | bytes 294920 | tf_op jit(solution)/shard_map/ppermute | solution.py:341
  59.0 10.0 %copy-start.8 = (f32[8,7,7]{2,0,1:T(8,128)S(1)}, f32[8,7,7]{2,0,1:T(8,128)}, u32[]{:S(2)}) copy-start(f32[8,7,7]{2,0,1:T(8,128)} %param.16) | copy-start | bytes 4708
  60.3 16.0 %copy-start.3 = (f32[8,3,8,128]{3,2,1,0:T(8,128)}, f32[8,3,8,128]{3,2,1,0:T(8,128)S(1)}, u32[]{:S(2)}) copy-start(f32[8,3,8,128]{3,2,1,0:T(8,128)S(1)} %collective-permute-done.8.side0_ref) | copy-start | bytes 294916
  63.6 12.8 %copy-start.4 = (f32[8,3,8,128]{3,2,1,0:T(8,128)}, f32[8,3,8,128]{3,2,1,0:T(8,128)S(1)}, u32[]{:S(2)}) copy-start(f32[8,3,8,128]{3,2,1,0:T(8,128)S(1)} %collective-permute-done.9.side1_ref) | copy-start | bytes 294916
  63.7 12.7 %collective-permute-start.11 = (f32[2,560,128]{2,1,0:T(8,128)S(1)}, f32[2,560,128]{2,1,0:T(8,128)S(1)}, u32[]{:S(2)}, u32[]{:S(2)}) collective-permute-start(f32[2,560,128]{2,1,0:T(8,128)S(1)} %get-tuple-element.17), channel_id=1, source_target_pairs={{8,16},{16,8},{9,17},{17,9},{10,18},{18,10},{11,19},{19,11},{12,20... | collective-permute-start | bytes 1720328 | tf_op jit(solution)/shard_map/ppermute | solution.py:341
  69.0 7.4 %collective-permute-start.10 = (f32[2,560,128]{2,1,0:T(8,128)S(1)}, f32[2,560,128]{2,1,0:T(8,128)S(1)}, u32[]{:S(2)}, u32[]{:S(2)}) collective-permute-start(f32[2,560,128]{2,1,0:T(8,128)S(1)} %get-tuple-element.18), channel_id=1, source_target_pairs={{0,8},{16,24},{8,0},{24,16},{1,9},{17,25},{9,1},{25,17},{2,10},{18... | collective-permute-start | bytes 1720328 | tf_op jit(solution)/shard_map/ppermute | solution.py:341
  76.4 0.8 copy-start
  77.2 0.8 copy-start.1

commit v3 on v2

--- a/solution.py
+++ b/solution.py
@@ -111,9 +111,38 @@
     return kept, other, rows(kept, 1), rows(other, 1)
 
 
-def main_kernel(
+def update(x, taper, spread_w, gain_w):
+    high, low_part = split(x)
+    c_high, c_low = split(dot(jnp.concatenate([high, low_part, high], 1), spread_w) * taper)
+    both = dot(c_high, gain_w)
+    lanes = 2 * MEMBERS
+    return x + (both[:, :lanes] + both[:, lanes:] + dot(c_low, gain_w[:, :lanes]))
+
+
+def load_pair(prior_ref, row, pair, lo, hi):
+    low = low_lanes((hi - lo, 2 * MEMBERS))
+    a = prior_ref[row, lo:hi, 128 * pair : 128 * (pair + 1)]
+    b = prior_ref[row + 1, lo:hi, 128 * pair : 128 * (pair + 1)]
+    return jnp.where(low, a, swap_halves(b)), jnp.where(low, swap_halves(a), b)
+
+
+def positions(start, length):
+    steps = lax.broadcasted_iota(jnp.int32, (length, OBS), 0)
+    return (start + steps).astype(F32) * (1.0 / HALFW)
+
+
+def pair_taper(first_row, gap, obs_row, active):
+    halves = []
+    for h in range(2):
+        dy = (first_row + h).astype(F32) * (1.0 / HALFW) - obs_row
+        halves.append(taper_weights(gap + dy * dy) * active)
+    return jnp.concatenate(halves, 1)
+
+
+def edge_kernel(
     width, order, cells, mask, cell_ref, value_ref, var_ref, prior_ref, p0, p1, p2, p3,
-    out_ref, first_ref, second_ref, predicted, table,
+    rows_ref, ends_ref, send0_ref, send1_ref, first_ref, second_ref, spread_ref, gain_ref,
+    place_ref, predicted, table,
 ):
     height, cols = prior_ref.shape[0], prior_ref.shape[1]
     my_row, my_col = lax.axis_index("rows"), lax.axis_index("cols")
@@ -122,13 +151,19 @@
     mine = 2 * lax.rem(my_row, 2) + lax.rem(lax.div(my_row, 2), 2)
     for rel, part in enumerate((p0, p1, p2, p3)):
         predicted[jnp.bitwise_xor(rel, mine)] = part[...]
-    low = low_lanes((cols, 2 * MEMBERS))
-    for j in range(height // 2):
-        for p in range(SPECIES // 2):
-            a = prior_ref[2 * j, :, 128 * p : 128 * (p + 1)]
-            b = prior_ref[2 * j + 1, :, 128 * p : 128 * (p + 1)]
-            out_ref[j, 2 * p * cols : (2 * p + 1) * cols] = jnp.where(low, a, swap_halves(b))
-            out_ref[j, (2 * p + 1) * cols : (2 * p + 2) * cols] = jnp.where(low, swap_halves(a), b)
+    pairs = height // 2
+    outer = (0, 1, pairs - 2, pairs - 1)
+    inner = tuple(range(2, pairs - 2))
+    for p in range(SPECIES // 2):
+        for i, j in enumerate(outer):
+            a, b = load_pair(prior_ref, 2 * j, p, 0, cols)
+            rows_ref[i, 2 * p * cols : (2 * p + 1) * cols] = a
+            rows_ref[i, (2 * p + 1) * cols : (2 * p + 2) * cols] = b
+        for i, j in enumerate(inner):
+            for side, lo in enumerate((0, cols - 8)):
+                a, b = load_pair(prior_ref, 2 * j, p, lo, lo + 8)
+                ends_ref[i, 2 * p, 8 * side : 8 * side + 8] = a
+                ends_ref[i, 2 * p + 1, 8 * side : 8 * side + 8] = b
     batches = [order[k] for k in range(BATCHES)]
     tiles = []
     for k in range(BATCHES):
@@ -141,20 +176,14 @@
     row_lane = jnp.floor(cell_lane * (1.0 / width))
     col_lane = (cell_lane - row_lane * width) * (1.0 / HALFW)
     row_lane = row_lane * (1.0 / HALFW)
+    place_ref[0:8, :] = row_lane
+    place_ref[8:16, :] = col_lane
     row_col = jnp.transpose(row_lane)
     col_col = jnp.transpose(col_lane)
     value_col = jnp.transpose(table[8:16, :])
     var_col = jnp.transpose(table[16:24, :])
     low_obs = low_lanes((OBS, 2 * MEMBERS))
-    x_pos = (my_col * cols + lax.broadcasted_iota(jnp.int32, (cols, OBS), 0)).astype(F32) * (
-        1.0 / HALFW
-    )
-
-    def update(x, taper, spread_w, gain_w, gain_hi):
-        high, low_part = split(x)
-        c_high, c_low = split(dot(jnp.concatenate([high, low_part, high], 1), spread_w) * taper)
-        both = dot(c_high, gain_w)
-        return x + (both[:, : 2 * MEMBERS] + both[:, 2 * MEMBERS :] + dot(c_low, gain_hi))
+    x_pos = positions(my_col * cols, cols)
 
     for k in range(BATCHES):
         block = predicted[k % 4]
@@ -178,8 +207,9 @@
         wide_hi, wide_lo = split(wide)
         spread_w = jnp.concatenate([wide_hi, wide_hi, wide_lo], 0)
         tall = jnp.concatenate([jnp.where(low_obs, gain, zero), jnp.where(low_obs, zero, gain)], 0)
-        tall_hi, tall_lo = split(tall)
-        gain_w = jnp.concatenate([tall_hi, tall_lo], 1)
+        gain_w = jnp.concatenate(split(tall), 1)
+        spread_ref[k] = spread_w
+        gain_ref[k] = gain_w
         obs_row, obs_col = row_lane[k : k + 1, :], col_lane[k : k + 1, :]
         if k < BATCHES - 1:
             for q in range(4):
@@ -191,65 +221,131 @@
                     dc = col_col[:, later : later + 1] - obs_col
                     active = (mask[batches[k], tiles[later]] > 0).astype(F32)
                     halves.append(taper_weights(dr * dr + dc * dc) * active)
-                predicted[q] = update(
-                    predicted[q], jnp.concatenate(halves, 1), spread_w, gain_w, tall_hi
-                )
-
+                predicted[q] = update(predicted[q], jnp.concatenate(halves, 1), spread_w, gain_w)
         active = (mask[batches[k], my_tile] > 0).astype(F32)
-        dx = x_pos - obs_col
-        dx = dx * dx
-        for j in range(height // 2):
-            halves = []
-            for h in range(2):
-                dy = (my_row * height + 2 * j + h).astype(F32) * (1.0 / HALFW) - obs_row
-                halves.append(taper_weights(dx + dy * dy) * active)
-            taper = jnp.concatenate([jnp.concatenate(halves, 1)] * SPECIES, 0)
-            out_ref[j] = update(out_ref[j], taper, spread_w, gain_w, tall_hi)
-
+        gap = x_pos - obs_col
+        gap = gap * gap
+        for i, j in enumerate(outer):
+            taper = pair_taper(my_row * height + 2 * j, gap, obs_row, active)
+            rows_ref[i] = update(
+                rows_ref[i], jnp.concatenate([taper] * SPECIES, 0), spread_w, gain_w
+            )
+        gap = jnp.concatenate([gap[:8], gap[cols - 8 :]], 0)
+        tapers = []
+        for j in inner:
+            tapers += [pair_taper(my_row * height + 2 * j, gap, obs_row, active)] * SPECIES
+        flat = (len(inner) * SPECIES * 16, 2 * MEMBERS)
+        ends = update(ends_ref[...].reshape(flat), jnp.concatenate(tapers, 0), spread_w, gain_w)
+        ends_ref[...] = ends.reshape(ends_ref.shape)
+
+    even = lax.rem(my_row, 2) == 0
+    low = low_lanes((cols, 2 * MEMBERS))
+    for t in range(SPECIES):
+        lo, hi = t * cols, (t + 1) * cols
+        top, bottom = rows_ref[0, lo:hi, :], rows_ref[3, lo:hi, :]
+        send0_ref[lo:hi, :] = jnp.where(even, bottom, top)
+        send1_ref[lo:hi, :] = jnp.where(even, top, bottom)
+    base = SPECIES * cols
+    for p in range(SPECIES // 2):
+        a, b = slice(2 * p * cols, (2 * p + 1) * cols), slice((2 * p + 1) * cols, (2 * p + 2) * cols)
+        top = jnp.where(low, rows_ref[1, a, :], swap_halves(rows_ref[1, b, :]))
+        bottom = jnp.where(low, swap_halves(rows_ref[2, a, :]), rows_ref[2, b, :])
+        lo, hi = base + p * cols, base + (p + 1) * cols
+        send0_ref[lo:hi, :] = jnp.where(even, bottom, top)
+        send1_ref[lo:hi, :] = jnp.where(even, top, bottom)
     even = lax.rem(my_col, 2) == 0
-    for j in range(height // 2):
-        for e in range(HALO):
-            for t in range(SPECIES):
-                r = t * cols + e
-                a = out_ref[j, r : r + 1, :]
-                r = t * cols + cols - HALO + e
-                b = out_ref[j, r : r + 1, :]
-                first_ref[j, e, t : t + 1, :] = jnp.where(even, b, a)
-                second_ref[j, e, t : t + 1, :] = jnp.where(even, a, b)
+    for j in range(pairs):
+        for t in range(SPECIES):
+            if j in outer:
+                i = outer.index(j)
+                a = rows_ref[i, t * cols : t * cols + HALO, :]
+                b = rows_ref[i, (t + 1) * cols - HALO : (t + 1) * cols, :]
+            else:
+                a = ends_ref[j - 2, t, 0:HALO, :]
+                b = ends_ref[j - 2, t, 16 - HALO : 16, :]
+            first_ref[j * SPECIES + t] = jnp.where(even, b, a)
+            second_ref[j * SPECIES + t] = jnp.where(even, a, b)
+
+
+def inner_kernel(first_row, height, order, mask, prior_ref, spread_ref, gain_ref, place_ref, out_ref):
+    cols = prior_ref.shape[1]
+    across = lax.axis_size("cols")
+    my_row, my_col = lax.axis_index("rows"), lax.axis_index("cols")
+    my_tile = my_row * across + my_col
+    pairs = out_ref.shape[0]
+    for j in range(pairs):
+        for p in range(SPECIES // 2):
+            a, b = load_pair(prior_ref, 2 * j, p, 8, cols - 8)
+            out_ref[j, 2 * p] = a
+            out_ref[j, 2 * p + 1] = b
+    x_pos = positions(my_col * cols + 8, cols - 16)
+    flat = (SPECIES * (cols - 16), 2 * MEMBERS)
+    for k in range(BATCHES):
+        active = (mask[order[k], my_tile] > 0).astype(F32)
+        obs_row = place_ref[k : k + 1, :]
+        gap = x_pos - place_ref[8 + k : 9 + k, :]
+        gap = gap * gap
+        spread_w, gain_w = spread_ref[k], gain_ref[k]
+        for j in range(pairs):
+            taper = pair_taper(my_row * height + first_row + 2 * j, gap, obs_row, active)
+            taper = jnp.concatenate([taper] * SPECIES, 0)
+            new = update(out_ref[j].reshape(flat), taper, spread_w, gain_w)
+            out_ref[j] = new.reshape(SPECIES, cols - 16, 2 * MEMBERS)
 
 
 def smooth_kernel(
-    kern, mix, tile_ref, side0_ref, side1_ref, rows0_ref, rows1_ref, out_ref, padded, lines
+    kern, mix, rows_ref, ends_ref, mid0_ref, mid1_ref, side0_ref, side1_ref, rows0_ref, rows1_ref,
+    out_ref, padded, lines,
 ):
-    pairs, cols = tile_ref.shape[0], tile_ref.shape[1] // SPECIES
+    cols = mid0_ref.shape[2] + 16
+    inner = ends_ref.shape[0]
+    pairs = inner + 4
     depth = cols + 16
     lanes = 2 * MEMBERS
     even_row = lax.rem(lax.axis_index("rows"), 2) == 0
     even_col = lax.rem(lax.axis_index("cols"), 2) == 0
     edge = jnp.zeros((8, lanes), F32)
+    own = pairs * SPECIES
+    packed = SPECIES + SPECIES // 2
+    above = jnp.where(even_row, own + packed, own)
+    below = jnp.where(even_row, own, own + packed)
 
     for q in range(pairs + 4):
-        inside = 2 <= q < pairs + 2
-        p = q - 2 if inside else (q if q < 2 else q - pairs - 2)
-
-        def outside(lo, hi):
-            a, b = rows0_ref[p, lo:hi, :], rows1_ref[p, lo:hi, :]
-            return jnp.where(even_row, b, a) if q < 2 else jnp.where(even_row, a, b)
-
+        p = q - 2
         for t in range(SPECIES):
             padded[q, t, 0:8, :] = edge
             padded[q, t, depth - 8 : depth, :] = edge
-            lo, hi = t * cols, (t + 1) * cols
-            padded[q, t, 8 : 8 + cols, :] = tile_ref[p, lo:hi, :] if inside else outside(lo, hi)
-            for e in range(HALO):
-                if inside:
-                    a, b = side0_ref[p, e, t : t + 1, :], side1_ref[p, e, t : t + 1, :]
+            if 0 <= p < pairs:
+                at = p * SPECIES + t
+                if p < 2 or p >= pairs - 2:
+                    i = p if p < 2 else p - pairs + 4
+                    padded[q, t, 8 : 8 + cols, :] = rows_ref[i, t * cols : (t + 1) * cols, :]
                 else:
-                    at = SPECIES * cols + e * SPECIES + t
-                    a = outside(at, at + 1)
-                    b = outside(at + HALO * SPECIES, at + HALO * SPECIES + 1)
-                padded[q, t, 5 + e : 6 + e, :] = jnp.where(even_col, b, a)
-                padded[q, t, 8 + cols + e : 9 + cols + e, :] = jnp.where(even_col, a, b)
+                    i = p - 2
+                    mid = mid0_ref if i < inner // 2 else mid1_ref
+                    padded[q, t, 8:16, :] = ends_ref[i, t, 0:8, :]
+                    padded[q, t, 16:cols, :] = mid[i % (inner // 2), t]
+                    padded[q, t, cols : cols + 8, :] = ends_ref[i, t, 8:16, :]
+
+                def unpack(x):
+                    return x
+
+            else:
+                base = above if q < 2 else below
+                whole = q in (1, pairs + 2)
+                at = base + t if whole else base + SPECIES + t // 2
+                lo = t * cols if whole else (SPECIES + t // 2) * cols
+                a, b = rows0_ref[lo : lo + cols, :], rows1_ref[lo : lo + cols, :]
+                body = jnp.where(even_row, b, a) if q < 2 else jnp.where(even_row, a, b)
+
+                def unpack(x):
+                    wanted = 1 if q < 2 else 0
+                    return x if whole or t % 2 == wanted else swap_halves(x)
+
+                padded[q, t, 8 : 8 + cols, :] = unpack(body)
+            a, b = side0_ref[at], side1_ref[at]
+            padded[q, t, 5:8, :] = unpack(jnp.where(even_col, b, a))
+            padded[q, t, 8 + cols : 11 + cols, :] = unpack(jnp.where(even_col, a, b))
     column = lax.broadcasted_iota(jnp.int32, (cols, 3 * depth), 1)
     third = column >= 2 * depth
     column = jnp.where(third, column - 2 * depth, jnp.where(column >= depth, column - depth, column))
@@ -321,41 +417,69 @@
         name="gather",
     )(batch_order, obs_cell, jnp.transpose(obs_weight, (0, 2, 1)), prior)
     arrived = exchange(kept, sent)
-    tile, first, second = pl.pallas_call(
-        functools.partial(main_kernel, width),
+    inner = pairs - 4
+    f32 = lambda *shape: jax.ShapeDtypeStruct(shape, F32)
+    rows, ends, send0, send1, first, second, spread, gain, place = pl.pallas_call(
+        functools.partial(edge_kernel, width),
         out_shape=(
-            jax.ShapeDtypeStruct((pairs, SPECIES * cols, lanes), F32),
-            jax.ShapeDtypeStruct((pairs, HALO, SPECIES, lanes), F32),
-            jax.ShapeDtypeStruct((pairs, HALO, SPECIES, lanes), F32),
+            f32(4, SPECIES * cols, lanes),
+            f32(inner, SPECIES, 16, lanes),
+            f32((SPECIES + SPECIES // 2) * cols, lanes),
+            f32((SPECIES + SPECIES // 2) * cols, lanes),
+            f32(pairs * SPECIES, HALO, lanes),
+            f32(pairs * SPECIES, HALO, lanes),
+            jax.ShapeDtypeStruct((BATCHES, 3 * lanes, 2 * OBS), BF16),
+            jax.ShapeDtypeStruct((BATCHES, 2 * OBS, 2 * lanes), BF16),
+            f32(2 * BATCHES, OBS),
         ),
         in_specs=[SMEM] * 3 + [VMEM] * 8,
-        out_specs=(VMEM, VMEM, VMEM),
+        out_specs=(VMEM,) * 9,
         scratch_shapes=[pltpu.VMEM((4, OBS, lanes), F32), pltpu.VMEM((24, OBS), F32)],
         compiler_params=PARAMS,
-        name="assimilate",
+        name="edges",
     )(batch_order, obs_cell, loc_mask, obs_cell, obs_value, obs_var, prior, *arrived)
+
+    def middle(part):
+        count = inner // 2
+        block = 2 * count
+        index = 4 // block + part
+        return pl.pallas_call(
+            functools.partial(inner_kernel, 4 + block * part, height),
+            out_shape=f32(count, SPECIES, cols - 16, lanes),
+            grid=(1,),
+            in_specs=[SMEM, SMEM, pl.BlockSpec((block, cols, channels), lambda i: (index, 0, 0))]
+            + [VMEM] * 3,
+            out_specs=VMEM,
+            compiler_params=PARAMS,
+            name="inner",
+        )(batch_order, loc_mask, prior, spread, gain, place)
 
     def swap(x, axis, start):
         size = lax.axis_size(axis)
         pairs_of = [(i, i + 1) for i in range(start, size - 1, 2)]
         return lax.ppermute(x, axis, pairs_of + [(j, i) for i, j in pairs_of])
 
-    side0, side1 = swap(first, "cols", 0), swap(second, "cols", 1)
-
-    def with_sides(lo, hi):
-        flat = (hi - lo, HALO * SPECIES, lanes)
-        return jnp.concatenate(
-            [tile[lo:hi], side0[lo:hi].reshape(flat), side1[lo:hi].reshape(flat)], 1
-        )
-
-    even = lax.rem(lax.axis_index("rows"), 2) == 0
-    bottom, top = with_sides(pairs - 2, pairs), with_sides(0, 2)
-    rows0 = swap(jnp.where(even, bottom, top), "rows", 0)
-    rows1 = swap(jnp.where(even, top, bottom), "rows", 1)
+    rows1 = swap(send1, "rows", 1)
+    rows0 = swap(send0, "rows", 0)
+    mid0 = middle(0)
+    rows0, rows1, mid0 = lax.optimization_barrier((rows0, rows1, mid0))
+    even = lax.rem(lax.axis_index("cols"), 2) == 0
+
+    def corner(x, at_right):
+        strips = x.reshape(SPECIES + SPECIES // 2, cols, lanes)
+        return jnp.where(at_right, strips[:, cols - HALO :], strips[:, :HALO])
+
+    first = jnp.concatenate([first, corner(rows0, even), corner(rows1, even)], 0)
+    odd = jnp.logical_not(even)
+    second = jnp.concatenate([second, corner(rows0, odd), corner(rows1, odd)], 0)
+    side1 = swap(second, "cols", 1)
+    side0 = swap(first, "cols", 0)
+    mid1 = middle(1)
+    side0, side1, mid1 = lax.optimization_barrier((side0, side1, mid1))
     return pl.pallas_call(
         smooth_kernel,
         out_shape=jax.ShapeDtypeStruct((height, cols, channels), F32),
-        in_specs=[SMEM, SMEM] + [VMEM] * 5,
+        in_specs=[SMEM, SMEM] + [VMEM] * 8,
         out_specs=VMEM,
         scratch_shapes=[
             pltpu.VMEM((pairs + 4, SPECIES, cols + 16, lanes), F32),
@@ -363,7 +487,7 @@
         ],
         compiler_params=PARAMS,
         name="smooth",
-    )(kernel.reshape(SPECIES, KW * KW), mixing, tile, side0, side1, rows0, rows1)
+    )(kernel.reshape(SPECIES, KW * KW), mixing, rows, ends, mid0, mid1, side0, side1, rows0, rows1)
 
 
 def solution(mesh):

time: 90.8 us -> 86.5 us (0.953)
  waiting for transfers between devices: 22.7 us -> 10.9 us
  Pallas kernels: 39.8 us -> 45.1 us
  starting transfers between devices: 21.6 us -> 26.4 us
  local copies, waits for them, and re-layouts: 4.22 us -> 2.06 us
    ppermute x4, waiting for transfers between devices: 9.84 us -> 0.69 us  [swap(): return lax.ppermute(x, axis, pairs_of + [(j, i) for i, j in pairs_of])]
    pallas_call x1 -> x3, Pallas kernels: 24.3 us -> 31.2 us  [the longest x1 18 us: shards(): pl.pallas_call(functools.partial(edge_kernel, width), out_shape=(f32(4, S...]
    ppermute x3, starting transfers between devices: 2.25 us -> 7.12 us  [exchange(): lax.ppermute(kept, 'cols', [(i, i ^ bit) for i in range(cols)])]
    ppermute x3, waiting for transfers between devices: 8.2 us -> 6.25 us  [exchange(): lax.ppermute(kept, 'cols', [(i, i ^ bit) for i in range(cols)])]
    pallas_call x1, Pallas kernels: 4.13 us -> 2.63 us  [shards(): pl.pallas_call(functools.partial(gather_kernel, width), out_shape=(jax.Sh...]
    slice x1 -> x0, local copies, waits for them, and re-layouts: 1.27 us -> none  [with_sides(): tile[lo:hi]]
    unnamed x19 -> x23, local copies, waits for them, and re-layouts: 2.27 us -> 1.39 us
  transfers between devices with their start and end apart: 12 -> 12, of which waited for: 8 -> 7; matrix products, arithmetic and copies ran while one was open for 2% -> 1% of each run, Pallas kernels for 0% -> 15%
where the time goes in v3:
time: 86.5 us; the launch traced here: 85.7 us
  Pallas kernels  45.1 us (52%)
  starting transfers between devices  26.4 us (31%)
  waiting for transfers between devices  10.9 us (13%)
  local copies, waits for them, and re-layouts  2.06 us (2%)
  other arithmetic  1.07 us (1%)
    pallas_call x1, Pallas kernels, shards(): pl.pallas_call(functools.partial(edge_kernel, width), out_shape=(f32(4, S...  18 us
    pallas_call x2, Pallas kernels, middle(): pl.pallas_call(functools.partial(inner_kernel, 4 + block * part, height),...  13.2 us
    pallas_call x1, Pallas kernels, shards(): pl.pallas_call(smooth_kernel, out_shape=jax.ShapeDtypeStruct((height, col...  11.3 us
    ppermute x5, starting transfers between devices, rows(): return lax.ppermute(x, 'rows', [(i, i ^ bit) for i in range(size)])  10.4 us
    ppermute x4, starting transfers between devices, swap(): return lax.ppermute(x, axis, pairs_of + [(j, i) for i, j in pairs_of])  8.87 us
    ppermute x3, starting transfers between devices, exchange(): lax.ppermute(kept, 'cols', [(i, i ^ bit) for i in range(cols)])  7.12 us
    ppermute x3, waiting for transfers between devices, exchange(): lax.ppermute(kept, 'cols', [(i, i ^ bit) for i in range(cols)])  6.25 us
    ppermute x5, waiting for transfers between devices, rows(): return lax.ppermute(x, 'rows', [(i, i ^ bit) for i in range(size)])  3.98 us
  transfers between devices with their start and end apart: 12, of which 7 were waited for; matrix products, arithmetic and copies ran while one was open for 1% of the time, Pallas kernels for 15%

profile of v3, /device:TPU:9, one launch (start us, length us, event | category | flops | bytes accessed | tf_op | source)
XLA Modules:
  0.0 85.7 jit_solution(360756860471070632)
XLA Ops:
  0.0 2.6 %gather.1 = (f32[2,128,128]{2,1,0:T(8,128)}, f32[2,128,128]{2,1,0:T(8,128)}) custom-call(s32[8]{0:T(128)} %order.7, s32[8,128]{1,0:T(8,128)} %cell_ref.1, f32[8,8,128]{2,1,0:T(8,128)} %bitcast.11, f32[16,64,512]{2,1,0:T(8,128)} %prior_ref.7), custom_call_target="tpu_custom_call" | custom-call | tf_op jit(solution)/shard_map/gather/pallas_call | solution.py:410
  2.6 0.7 collective-permute-start
  3.3 1.2 %collective-permute-done = f32[2,128,128]{2,1,0:T(8,128)S(1)} collective-permute-done((f32[2,128,128]{2,1,0:T(8,128)}, f32[2,128,128]{2,1,0:T(8,128)S(1)}, u32[]{:S(2)}, u32[]{:S(2)}) %collective-permute-start) | collective-permute-done | bytes 131104 | tf_op jit(solution)/shard_map/ppermute | solution.py:98
  4.5 0.9 %add.15 = f32[2,128,128]{2,1,0:T(8,128)S(1)} add(f32[2,128,128]{2,1,0:T(8,128)} %get-tuple-element.22, f32[2,128,128]{2,1,0:T(8,128)S(1)} %collective-permute-done) | non-fusion elementwise | flops 32768 | bytes 393216 | tf_op jit(solution)/shard_map/add | solution.py:100
  5.4 1.3 %collective-permute-start.1 = (f32[128,128]{1,0:T(8,128)S(1)}, f32[128,128]{1,0:T(8,128)S(1)}, u32[]{:S(2)}, u32[]{:S(2)}) collective-permute-start(f32[128,128]{1,0:T(8,128)S(1)} %slice_bitcast_fusion), channel_id=1, source_target_pairs={{0,16},{8,24},{16,0},{24,8},{1,17},{9,25},{17,1},{25,9},{2,18},{10... | collective-permute-start | bytes 196616 | tf_op jit(solution)/shard_map/ppermute | solution.py:98
  6.8 1.9 %collective-permute-done.1 = f32[128,128]{1,0:T(8,128)S(1)} collective-permute-done((f32[128,128]{1,0:T(8,128)S(1)}, f32[128,128]{1,0:T(8,128)S(1)}, u32[]{:S(2)}, u32[]{:S(2)}) %collective-permute-start.1) | collective-permute-done | bytes 65568 | tf_op jit(solution)/shard_map/ppermute | solution.py:98
  8.6 1.3 %collective-permute-start.2 = (f32[128,128]{1,0:T(8,128)S(1)}, f32[128,128]{1,0:T(8,128)S(1)}, u32[]{:S(2)}, u32[]{:S(2)}) collective-permute-start(f32[128,128]{1,0:T(8,128)S(1)} %fusion), channel_id=1, source_target_pairs={{0,1},{1,0},{2,3},{3,2},{4,5},{5,4},{6,7},{7,6},{8,9},{9,8},{10,11... | collective-permute-start | bytes 196616 | tf_op jit(solution)/shard_map/ppermute | solution.py:108
  9.9 1.9 %collective-permute-done.2 = f32[128,128]{1,0:T(8,128)S(1)} collective-permute-done((f32[128,128]{1,0:T(8,128)S(1)}, f32[128,128]{1,0:T(8,128)S(1)}, u32[]{:S(2)}, u32[]{:S(2)}) %collective-permute-start.2) | collective-permute-done | bytes 65568 | tf_op jit(solution)/shard_map/ppermute | solution.py:108
  11.8 0.5 collective-permute-start.3
  12.4 2.6 %collective-permute-done.3 = f32[128,128]{1,0:T(8,128)S(1)} collective-permute-done((f32[128,128]{1,0:T(8,128)S(1)}, f32[128,128]{1,0:T(8,128)S(1)}, u32[]{:S(2)}, u32[]{:S(2)}) %collective-permute-start.3) | collective-permute-done | bytes 65568 | tf_op jit(solution)/shard_map/ppermute | solution.py:108
  15.0 5.3 %collective-permute-start.4 = (f32[128,128]{1,0:T(8,128)S(1)}, f32[128,128]{1,0:T(8,128)S(1)}, u32[]{:S(2)}, u32[]{:S(2)}) collective-permute-start(f32[128,128]{1,0:T(8,128)S(1)} %add.18), channel_id=1, source_target_pairs={{0,4},{1,5},{2,6},{3,7},{4,0},{5,1},{6,2},{7,3},{8,12},{9,13},{10,... | collective-permute-start | bytes 196616 | tf_op jit(solution)/shard_map/ppermute | solution.py:108
  20.3 1.7 %collective-permute-done.4 = f32[128,128]{1,0:T(8,128)S(1)} collective-permute-done((f32[128,128]{1,0:T(8,128)S(1)}, f32[128,128]{1,0:T(8,128)S(1)}, u32[]{:S(2)}, u32[]{:S(2)}) %collective-permute-start.4) | collective-permute-done | bytes 65568 | tf_op jit(solution)/shard_map/ppermute | solution.py:108
  22.1 0.8 collective-permute-start.5
  22.9 3.5 %collective-permute-start.6 = (f32[128,128]{1,0:T(8,128)S(1)}, f32[128,128]{1,0:T(8,128)S(1)}, u32[]{:S(2)}, u32[]{:S(2)}) collective-permute-start(f32[128,128]{1,0:T(8,128)S(1)} %add.19.p0), channel_id=1, source_target_pairs={{0,8},{8,0},{16,24},{24,16},{1,9},{9,1},{17,25},{25,17},{2,10},{10... | collective-permute-start | bytes 196616 | tf_op jit(solution)/shard_map/ppermute | solution.py:98
  26.4 0.0 collective-permute-done.5.p1
  26.4 4.1 %collective-permute-start.7 = (f32[128,128]{1,0:T(8,128)S(1)}, f32[128,128]{1,0:T(8,128)S(1)}, u32[]{:S(2)}, u32[]{:S(2)}) collective-permute-start(f32[128,128]{1,0:T(8,128)S(1)} %collective-permute-done.5.p1), channel_id=1, source_target_pairs={{0,8},{8,0},{16,24},{24,16},{1,9},{9,1},{17,25},{25,17},{2,10},{10... | collective-permute-start | bytes 196616 | tf_op jit(solution)/shard_map/ppermute | solution.py:98
  30.5 0.0 collective-permute-done.6.p2
  30.5 0.9 %collective-permute-done.7.p3 = f32[128,128]{1,0:T(8,128)S(1)} collective-permute-done((f32[128,128]{1,0:T(8,128)S(1)}, f32[128,128]{1,0:T(8,128)S(1)}, u32[]{:S(2)}, u32[]{:S(2)}) %collective-permute-start.7) | collective-permute-done | bytes 65568 | tf_op jit(solution)/shard_map/ppermute | solution.py:98
  31.4 0.6 copy-done.9
  32.0 18.0 %edges.1 = (f32[4,512,128]{2,1,0:T(8,128)}, f32[4,8,16,128]{3,2,1,0:T(8,128)}, f32[768,128]{1,0:T(8,128)}, f32[768,128]{1,0:T(8,128)}, f32[64,3,128]{2,1,0:T(4,1...) custom-call(s32[8]{0:T(128)} %order.7, ...), custom_call_target="tpu_custom_call" | custom-call | tf_op jit(solution)/shard_map/edges/pallas_call | solution.py:422
  50.0 0.4 collective-permute-start.8
  50.3 1.9 %collective-permute-start.9 = (f32[768,128]{1,0:T(8,128)}, f32[768,128]{1,0:T(8,128)S(1)}, u32[]{:S(2)}, u32[]{:S(2)}) collective-permute-start(f32[768,128]{1,0:T(8,128)} %get-tuple-element.27), channel_id=1, source_target_pairs={{8,16},{16,8},{9,17},{17,9},{10,18},{18,10},{11,19},{19,11},{12,20... | collective-permute-start | bytes 1179656 | tf_op jit(solution)/shard_map/ppermute | solution.py:460
  52.3 0.0 copy-start.10
  52.3 6.6 %inner.2.mid0_ref = f32[2,8,48,128]{3,2,1,0:T(8,128)} custom-call(s32[8]{0:T(128)} %order.7, s32[8,32]{1,0:T(8,128)} %mask.5, f32[16,64,512]{2,1,0:T(8,128)} %prior_ref.7, bf16[8,384,256]{2,1,0:T(8,128)(2,1)} %get-tuple-element.28.spread_ref, bf16[8,256,256]{2,1,0:T(8,128)(2,1)} %get-tuple-element.29.gain_ref, f32[16,128]{1,0:T(8,128)} %get-tuple-element.30.place_ref), custom_call_target="tpu_custom_call" | custom-call | tf_op jit(solution)/shard_map/inner/pallas_call | solution.py:446
  58.9 0.7 collective-permute-done.9.rows1_ref
  59.7 5.5 %collective-permute-start.11 = (f32[88,3,128]{2,1,0:T(4,128)S(1)}, f32[88,3,128]{2,1,0:T(4,128)S(1)}, u32[]{:S(2)}, u32[]{:S(2)}) collective-permute-start(f32[88,3,128]{2,1,0:T(4,128)S(1)} %pad_maximum_fusion.1), channel_id=1, source_target_pairs={{1,2},{3,4},{5,6},{2,1},{4,3},{6,5},{9,10},{11,12},{13,14},{10,9},... | collective-permute-start | bytes 405512 | tf_op jit(solution)/shard_map/ppermute | solution.py:460
  65.3 1.1 %collective-permute-start.10 = (f32[88,3,128]{2,1,0:T(4,128)S(1)}, f32[88,3,128]{2,1,0:T(4,128)S(1)}, u32[]{:S(2)}, u32[]{:S(2)}) collective-permute-start(f32[88,3,128]{2,1,0:T(4,128)S(1)} %pad_maximum_fusion), channel_id=1, source_target_pairs={{0,1},{2,3},{4,5},{6,7},{1,0},{3,2},{5,4},{7,6},{8,9},{10,11},{12,... | collective-permute-start | bytes 405512 | tf_op jit(solution)/shard_map/ppermute | solution.py:460
  66.4 0.7 reshape.11.kern
  67.1 6.6 %inner.3.mid1_ref = f32[2,8,48,128]{3,2,1,0:T(8,128)} custom-call(s32[8]{0:T(128)} %order.7, s32[8,32]{1,0:T(8,128)} %mask.5, f32[16,64,512]{2,1,0:T(8,128)} %prior_ref.7, bf16[8,384,256]{2,1,0:T(8,128)(2,1)} %get-tuple-element.28.spread_ref, bf16[8,256,256]{2,1,0:T(8,128)(2,1)} %get-tuple-element.29.gain_ref, f32[16,128]{1,0:T(8,128)} %get-tuple-element.30.place_ref), custom_call_target="tpu_custom_call" | custom-call | tf_op jit(solution)/shard_map/inner/pallas_call | solution.py:446
  73.7 0.6 copy-done.3
  74.3 0.1 copy-done.4
  74.4 11.3 %smooth.1 = f32[16,64,512]{2,1,0:T(8,128)} custom-call(f32[8,49]{1,0:T(8,128)} %reshape.11.kern, f32[8,8]{1,0:T(8,128)} %mix.1, f32[4,512,128]{2,1,0:T(8,128)} %get-tuple-element.24.rows_ref, f32[4,8,16,128]{3,2,1,0:T(8,128)} %get-tuple-element.25.ends_ref, f32[2,8,48,128]{3,2,1,0:T(8,128)} %inner.2.mid0_ref, f32[2,8,48,128]{3,2,1,0:T(8,128)} %inner.3.mid1_ref, ...), custom_call_target="tpu_custom_call" | custom-call | tf_op jit(solution)/shard_map/smooth/pallas_call | solution.py:479
  (30 shorter events, 0.2 us)
Async XLA Ops:
  2.6 1.9 %collective-permute-start = (f32[2,128,128]{2,1,0:T(8,128)}, f32[2,128,128]{2,1,0:T(8,128)S(1)}, u32[]{:S(2)}, u32[]{:S(2)}) collective-permute-start(f32[2,128,128]{2,1,0:T(8,128)} %get-tuple-element.23), channel_id=1, source_target_pairs={{0,8},{8,0},{16,24},{24,16},{1,9},{9,1},{17,25},{25,17},{2,10},{10... | collective-permute-start | bytes 393224 | tf_op jit(solution)/shard_map/ppermute | solution.py:98
  5.4 3.2 %collective-permute-start.1 = (f32[128,128]{1,0:T(8,128)S(1)}, f32[128,128]{1,0:T(8,128)S(1)}, u32[]{:S(2)}, u32[]{:S(2)}) collective-permute-start(f32[128,128]{1,0:T(8,128)S(1)} %slice_bitcast_fusion), channel_id=1, source_target_pairs={{0,16},{8,24},{16,0},{24,8},{1,17},{9,25},{17,1},{25,9},{2,18},{10... | collective-permute-start | bytes 196616 | tf_op jit(solution)/shard_map/ppermute | solution.py:98
  8.6 3.2 %collective-permute-start.2 = (f32[128,128]{1,0:T(8,128)S(1)}, f32[128,128]{1,0:T(8,128)S(1)}, u32[]{:S(2)}, u32[]{:S(2)}) collective-permute-start(f32[128,128]{1,0:T(8,128)S(1)} %fusion), channel_id=1, source_target_pairs={{0,1},{1,0},{2,3},{3,2},{4,5},{5,4},{6,7},{7,6},{8,9},{9,8},{10,11... | collective-permute-start | bytes 196616 | tf_op jit(solution)/shard_map/ppermute | solution.py:108
  11.8 3.2 %collective-permute-start.3 = (f32[128,128]{1,0:T(8,128)S(1)}, f32[128,128]{1,0:T(8,128)S(1)}, u32[]{:S(2)}, u32[]{:S(2)}) collective-permute-start(f32[128,128]{1,0:T(8,128)S(1)} %add.17), channel_id=1, source_target_pairs={{0,2},{1,3},{2,0},{3,1},{4,6},{5,7},{6,4},{7,5},{8,10},{9,11},{10,... | collective-permute-start | bytes 196616 | tf_op jit(solution)/shard_map/ppermute | solution.py:108
  15.0 7.0 %collective-permute-start.4 = (f32[128,128]{1,0:T(8,128)S(1)}, f32[128,128]{1,0:T(8,128)S(1)}, u32[]{:S(2)}, u32[]{:S(2)}) collective-permute-start(f32[128,128]{1,0:T(8,128)S(1)} %add.18), channel_id=1, source_target_pairs={{0,4},{1,5},{2,6},{3,7},{4,0},{5,1},{6,2},{7,3},{8,12},{9,13},{10,... | collective-permute-start | bytes 196616 | tf_op jit(solution)/shard_map/ppermute | solution.py:108
  22.1 9.3 %copy-start.2 = (f32[128,128]{1,0:T(8,128)}, f32[128,128]{1,0:T(8,128)S(1)}, u32[]{:S(2)}) copy-start(f32[128,128]{1,0:T(8,128)S(1)} %add.19.p0) | copy-start | bytes 196612
  22.1 4.3 %collective-permute-start.5 = (f32[128,128]{1,0:T(8,128)S(1)}, f32[128,128]{1,0:T(8,128)S(1)}, u32[]{:S(2)}, u32[]{:S(2)}) collective-permute-start(f32[128,128]{1,0:T(8,128)S(1)} %add.19.p0), channel_id=1, source_target_pairs={{0,16},{8,24},{16,0},{24,8},{1,17},{9,25},{17,1},{25,9},{2,18},{10... | collective-permute-start | bytes 196616 | tf_op jit(solution)/shard_map/ppermute | solution.py:98
  22.9 7.6 %collective-permute-start.6 = (f32[128,128]{1,0:T(8,128)S(1)}, f32[128,128]{1,0:T(8,128)S(1)}, u32[]{:S(2)}, u32[]{:S(2)}) collective-permute-start(f32[128,128]{1,0:T(8,128)S(1)} %add.19.p0), channel_id=1, source_target_pairs={{0,8},{8,0},{16,24},{24,16},{1,9},{9,1},{17,25},{25,17},{2,10},{10... | collective-permute-start | bytes 196616 | tf_op jit(solution)/shard_map/ppermute | solution.py:98
  26.4 5.0 %copy-start.7 = (f32[128,128]{1,0:T(8,128)}, f32[128,128]{1,0:T(8,128)S(1)}, u32[]{:S(2)}) copy-start(f32[128,128]{1,0:T(8,128)S(1)} %collective-permute-done.5.p1) | copy-start | bytes 196612
  26.4 5.0 %collective-permute-start.7 = (f32[128,128]{1,0:T(8,128)S(1)}, f32[128,128]{1,0:T(8,128)S(1)}, u32[]{:S(2)}, u32[]{:S(2)}) collective-permute-start(f32[128,128]{1,0:T(8,128)S(1)} %collective-permute-done.5.p1), channel_id=1, source_target_pairs={{0,8},{8,0},{16,24},{24,16},{1,9},{9,1},{17,25},{25,17},{2,10},{10... | collective-permute-start | bytes 196616 | tf_op jit(solution)/shard_map/ppermute | solution.py:98
  30.5 0.9 %copy-start.8 = (f32[128,128]{1,0:T(8,128)}, f32[128,128]{1,0:T(8,128)S(1)}, u32[]{:S(2)}) copy-start(f32[128,128]{1,0:T(8,128)S(1)} %collective-permute-done.6.p2) | copy-start | bytes 196612
  31.4 0.6 copy-start.9
  50.0 9.0 %collective-permute-start.8 = (f32[768,128]{1,0:T(8,128)}, f32[768,128]{1,0:T(8,128)S(1)}, u32[]{:S(2)}, u32[]{:S(2)}) collective-permute-start(f32[768,128]{1,0:T(8,128)} %get-tuple-element.26), channel_id=1, source_target_pairs={{0,8},{16,24},{8,0},{24,16},{1,9},{17,25},{9,1},{25,17},{2,10},{18... | collective-permute-start | bytes 1179656 | tf_op jit(solution)/shard_map/ppermute | solution.py:460
  50.3 9.3 %collective-permute-start.9 = (f32[768,128]{1,0:T(8,128)}, f32[768,128]{1,0:T(8,128)S(1)}, u32[]{:S(2)}, u32[]{:S(2)}) collective-permute-start(f32[768,128]{1,0:T(8,128)} %get-tuple-element.27), channel_id=1, source_target_pairs={{8,16},{16,8},{9,17},{17,9},{10,18},{18,10},{11,19},{19,11},{12,20... | collective-permute-start | bytes 1179656 | tf_op jit(solution)/shard_map/ppermute | solution.py:460
  52.3 7.4 %copy-start.6 = (f32[64,3,128]{2,1,0:T(4,128)S(1)}, f32[64,3,128]{2,1,0:T(4,128)}, u32[]{:S(2)}) copy-start(f32[64,3,128]{2,1,0:T(4,128)} %get-tuple-element.35) | copy-start | bytes 294916
  52.3 13.0 %copy-start.5 = (f32[64,3,128]{2,1,0:T(4,128)S(1)}, f32[64,3,128]{2,1,0:T(4,128)}, u32[]{:S(2)}) copy-start(f32[64,3,128]{2,1,0:T(4,128)} %get-tuple-element.32) | copy-start | bytes 294916
  52.3 14.1 %copy-start.10 = (f32[8,7,7]{2,0,1:T(8,128)S(1)}, f32[8,7,7]{2,0,1:T(8,128)}, u32[]{:S(2)}) copy-start(f32[8,7,7]{2,0,1:T(8,128)} %param.16) | copy-start | bytes 4708
  58.9 14.7 %copy-start = (f32[768,128]{1,0:T(8,128)}, f32[768,128]{1,0:T(8,128)S(1)}, u32[]{:S(2)}) copy-start(f32[768,128]{1,0:T(8,128)S(1)} %collective-permute-done.8.rows0_ref) | copy-start | bytes 1179652
  59.6 14.0 %copy-start.1 = (f32[768,128]{1,0:T(8,128)}, f32[768,128]{1,0:T(8,128)S(1)}, u32[]{:S(2)}) copy-start(f32[768,128]{1,0:T(8,128)S(1)} %collective-permute-done.9.rows1_ref) | copy-start | bytes 1179652
  59.7 13.9 %collective-permute-start.11 = (f32[88,3,128]{2,1,0:T(4,128)S(1)}, f32[88,3,128]{2,1,0:T(4,128)S(1)}, u32[]{:S(2)}, u32[]{:S(2)}) collective-permute-start(f32[88,3,128]{2,1,0:T(4,128)S(1)} %pad_maximum_fusion.1), channel_id=1, source_target_pairs={{1,2},{3,4},{5,6},{2,1},{4,3},{6,5},{9,10},{11,12},{13,14},{10,9},... | collective-permute-start | bytes 405512 | tf_op jit(solution)/shard_map/ppermute | solution.py:460
  65.3 8.4 %collective-permute-start.10 = (f32[88,3,128]{2,1,0:T(4,128)S(1)}, f32[88,3,128]{2,1,0:T(4,128)S(1)}, u32[]{:S(2)}, u32[]{:S(2)}) collective-permute-start(f32[88,3,128]{2,1,0:T(4,128)S(1)} %pad_maximum_fusion), channel_id=1, source_target_pairs={{0,1},{2,3},{4,5},{6,7},{1,0},{3,2},{5,4},{7,6},{8,9},{10,11},{12,... | collective-permute-start | bytes 405512 | tf_op jit(solution)/shard_map/ppermute | solution.py:460
  73.7 0.7 copy-start.3
  73.7 0.7 copy-start.4
